TPU v7x, 512 devices: a whole 4x4x16 slice. The times are simulated.
512 devices in a mesh: walk: 64 (over z, y), col: 8 (over x, core).
Axes of the slice: x: 4, y: 4, z: 16, core: 2. Of those that a mesh axis runs over, the one named last changes fastest.
Arguments:
- jacobian: float32 [384, 524288], P('walk', 'col'), may hold values from -25 to 25
- prev_update: float32 [8, 65536], P('col', 'walk'), may hold values from -6 to 6
- base_energy: float32 [384], P('walk'), may hold values from -6 to 6
- elec_pos: float32 [384, 3, 66], P('walk'), may hold values from -8 to 8
- atom_pos: float32 [3, 21], replicated, may hold values from -6 to 6
- quad_ratio: float32 [384, 21, 66, 12], P('walk'), may hold values from -1.2 to 1.2
- rotation: int32 [384, 66], P('walk'), may hold values from 0 to 15
- channels: int32 [21], replicated, may hold values from 1 to 3
- ecp_coef: float32 [21, 3], replicated, may hold values from 0.5 to 2
- ecp_expo: float32 [21, 3], replicated, may hold values from 0.2 to 2
Outputs:
- local_energy: float32 [384], P('walk')
- update: float32 [8, 65536], P('col', 'walk')
All inputs are finite; a program needn't handle non-finite values.
Results may differ from a plain program's by a relative error of at most 0.0003.
Values sent between devices are 32-bit elements; how exact they have to be, the bound alone decides.
No kernel may reach another device: no remote copies, remote signals or barrier semaphores. Data moves between devices by JAX's collectives and lax.ppermute only.
A program may use at most 64 MiB of HBM per device.

v0:
```python
import math

import jax
import jax.numpy as jnp
from jax import lax
from jax.sharding import PartitionSpec as P

NROT = 16


momentum = 0.9
damping = 0.1


def icosa_points():
    golden = (1.0 + math.sqrt(5.0)) / 2.0
    length = math.sqrt(1.0 + golden * golden)
    rows = []
    for first in (-1.0, 1.0):
        for second in (-golden, golden):
            rows.append((0.0, first / length, second / length))
            rows.append((first / length, second / length, 0.0))
            rows.append((second / length, 0.0, first / length))
    return jnp.asarray(rows, dtype=jnp.float32).T


def rotation_table(count):
    angle = jnp.arange(count, dtype=jnp.float32)
    turn_z = 2.0 * math.pi * angle / count
    turn_x = 0.9 * angle
    cz, sz = (jnp.cos(turn_z), jnp.sin(turn_z))
    cx, sx = (jnp.cos(turn_x), jnp.sin(turn_x))
    zeros = jnp.zeros_like(cz)
    matrix = jnp.stack(
        [
            jnp.stack([cz, -sz * cx, sz * sx], axis=-1),
            jnp.stack([sz, cz * cx, -cz * sx], axis=-1),
            jnp.stack([zeros, sx, cx], axis=-1),
        ],
        axis=1,
    )
    points = icosa_points()
    rotated = matrix[:, :, 0, None] * points[None, 0, :]
    rotated = rotated + matrix[:, :, 1, None] * points[None, 1, :]
    rotated = rotated + matrix[:, :, 2, None] * points[None, 2, :]
    return rotated.reshape(count, -1)


def nonlocal_energy(elec_pos, atom_pos, quad_ratio, rotation, channels, ecp_coef, ecp_expo):
    walkers, electrons = rotation.shape
    count = NROT
    table = rotation_table(count)
    onehot = (rotation[:, :, None] == jnp.arange(count, dtype=jnp.int32)[None, None, :]).astype(
        jnp.float32
    )
    rotated = jnp.einsum("wek,kf->wef", onehot, table, precision=lax.Precision.HIGHEST)
    rotated = rotated.reshape(walkers, electrons, 3, -1)
    diff = elec_pos[:, :, None, :] - atom_pos[None, :, :, None]
    dist2 = jnp.sum(diff * diff, axis=1)
    unit = diff / jnp.sqrt(dist2 + 0.01)[:, None, :, :]
    cosang = unit[:, 0, :, :, None] * rotated[:, None, :, 0, :]
    cosang = cosang + unit[:, 1, :, :, None] * rotated[:, None, :, 1, :]
    cosang = cosang + unit[:, 2, :, :, None] * rotated[:, None, :, 2, :]
    quad = quad_ratio.shape[-1]
    lmax = ecp_coef.shape[1]
    lower = jnp.ones_like(cosang)
    upper = cosang
    total = jnp.zeros((walkers,), jnp.float32)
    for level in range(lmax):
        if level == 0:
            poly = lower
        elif level == 1:
            poly = upper
        else:
            fresh = ((2 * level - 1) * cosang * upper - (level - 1) * lower) / level
            lower, upper = (upper, fresh)
            poly = fresh
        angular = jnp.sum(poly * quad_ratio, axis=-1) / quad
        active = (channels > level).astype(jnp.float32)
        radial = ecp_coef[None, :, level, None] * jnp.exp(-ecp_expo[None, :, level, None] * dist2)
        term = (2 * level + 1) * active[None, :, None] * radial * angular
        total = total + jnp.sum(term, axis=(1, 2))
    return total


def sum_pieces(first, second):
    first_sum, second_sum = lax.psum((first, second), ("walk", "col"))
    return (first_sum, second_sum)


def body(
    jacobian,
    prev_update,
    base_energy,
    elec_pos,
    atom_pos,
    quad_ratio,
    rotation,
    channels,
    ecp_coef,
    ecp_expo,
):
    energy_mine = base_energy + nonlocal_energy(
        elec_pos, atom_pos, quad_ratio, rotation, channels, ecp_coef, ecp_expo
    )
    columns = lax.all_to_all(jacobian, "walk", split_axis=1, concat_axis=0, tiled=True)
    walkers = columns.shape[0]
    params_total = columns.shape[1] * lax.axis_size("walk") * lax.axis_size("col")
    scale = 1.0 / params_total
    centred = columns - jnp.mean(columns, axis=0, keepdims=True)
    prev_mine = prev_update[0]
    gram_part = (
        jnp.dot(
            centred, centred.T, precision=lax.Precision.HIGHEST, preferred_element_type=jnp.float32
        )
        * scale
    )
    along_part = (
        jnp.dot(
            centred, prev_mine, precision=lax.Precision.HIGHEST, preferred_element_type=jnp.float32
        )
        * scale
    )
    extra = along_part[:, None]
    gram, extra_sum = sum_pieces(gram_part, extra)
    along = extra_sum[:, 0]
    energies = lax.all_gather(energy_mine, "walk", axis=0, tiled=True)
    eps = -(energies - jnp.mean(energies)) / math.sqrt(walkers)
    system = gram + damping * jnp.eye(walkers, dtype=jnp.float32)
    factor = jnp.linalg.cholesky(system)
    solved = jax.scipy.linalg.cho_solve((factor, True), eps - momentum * along)
    update_mine = (
        jnp.dot(
            solved, centred, precision=lax.Precision.HIGHEST, preferred_element_type=jnp.float32
        )
        + momentum * prev_mine
    )
    return (energy_mine, update_mine[None, :])


def solution(mesh):
    in_specs = (
        P("walk", "col"),
        P("col", "walk"),
        P("walk"),
        P("walk", None, None),
        P(),
        P("walk", None, None, None),
        P("walk", None),
        P(),
        P(),
        P(),
    )
    out_specs = (P("walk"), P("col", "walk"))
    return jax.shard_map(body, mesh=mesh, in_specs=in_specs, out_specs=out_specs, check_vma=False)
```

profile of v0, /device:TPU:1, one launch (start us, length us, event | category | flops | bytes accessed | tf_op | source)
XLA Modules:
  0.0 826.4 jit_solution(6028116304954348564)
XLA Ops:
  7.3 19.4 %all-to-all-start = ((f32[6,64,1024]{2,0,1:T(8,128)}), f32[6,64,1024]{2,0,1:T(8,128)S(1)}, u32[]{:S(2)}, u32[]{:S(2)}) async-start(f32[6,64,1024]{2,0,1:T(8,128)} %bitcast.162), calls=%async_computation | async-start | bytes 4194304 | tf_op jit(solution)/shard_map/all_to_all | solution.py:106
  27.3 0.1 mul.376
  27.6 0.1 mul.384
  27.8 0.1 mul.392
  27.9 0.1 mul.379
  28.0 0.1 mul.387
  28.1 0.1 mul.395
  28.3 0.1 copy.26
  28.4 1.3 dynamic-slice.3
  30.4 0.1 fusion.13
  30.6 0.2 fusion.28
  30.8 0.1 subtract_divide_fusion
  30.9 0.6 multiply_reduce_fusion
  31.5 0.3 multiply_reduce_fusion.2
  31.8 0.5 fusion.57
  32.3 187.9 %all-reduce.1 = f32[384]{0:T(512)S(1)} all-reduce(f32[384]{0:T(512)S(1)} %get-tuple-element.32), channel_id=1, replica_groups=mesh['walk'=64,'col'=8] {'walk'}, use_global_device_ids=true, to_apply=%add.1 | all-reduce | flops 384 | bytes 3072
  220.3 0.6 reduce_sum.89
  221.5 0.2 reduce_sum.88
  221.7 1.6 subtract_bitcast_fusion
  223.3 1.6 sub.49
  225.0 3.4 convolution_multiply_fusion
  228.4 1.4 convolution_reduce_fusion
  229.9 133.3 %psum.15 = f32[384,1]{0,1:T(1,128)S(1)} all-reduce(f32[384,1]{0,1:T(1,128)S(1)} %broadcast_in_dim.6), channel_id=1, replica_groups=mesh['walk'=64,'col'=8] {'walk','col'}, use_global_device_ids=true, to_apply=%region_16.17 | all-reduce | flops 384 | bytes 3072 | tf_op jit(solution)/shard_map/psum | solution.py:87
  363.3 355.0 %all-reduce.4.cloned.1.call-done = f32[384,384]{0,1:T(8,128)} async-done(((f32[384,384]{0,1:T(8,128)}), f32[384,384]{0,1:T(8,128)}) %all-reduce.4.cloned.1.call-update) | async-done | bytes 589840 | tf_op jit(solution)/shard_map/psum | solution.py:87
  718.2 1.2 select_add_fusion
  719.4 0.2 copy.29
  719.8 11.7 %cholesky.76 = f32[128,128]{1,0:T(8,128)S(1)} custom-call(f32[128,128]{1,0:T(8,128)S(1)} %cholesky.189), custom_call_target="Cholesky" | custom-call | tf_op jit(solution)/shard_map/jit(cholesky)/cholesky | solution.py:130
  731.5 9.8 %custom-call.26 = f32[1,128,128]{1,2,0:T(8,128)S(1)} custom-call(f32[1,128,128]{2,1,0:T(8,128)S(1)} %get-tuple-element.45), custom_call_target="InvertDiagBlocksLowerTriangular" | custom-call | tf_op jit(solution)/shard_map/jit(cholesky)/cholesky | solution.py:130
  741.3 0.3 fusion.17
  741.6 0.3 convolution_subtract_fusion
  741.9 0.1 copy.31
  742.0 0.1 copy.30
  742.1 11.7 %cholesky.160 = f32[128,128]{1,0:T(8,128)S(1)} custom-call(f32[128,128]{1,0:T(8,128)S(1)} %cholesky.193), custom_call_target="Cholesky" | custom-call | tf_op jit(solution)/shard_map/jit(cholesky)/cholesky | solution.py:130
  753.8 0.1 copy.32
  754.0 10.0 %custom-call.27 = f32[1,128,128]{1,2,0:T(8,128)S(1)} custom-call(f32[1,128,128]{2,1,0:T(8,128)S(1)} %get-tuple-element.43), custom_call_target="InvertDiagBlocksLowerTriangular" | custom-call | tf_op jit(solution)/shard_map/jit(cholesky)/cholesky | solution.py:130
  764.0 0.3 convolution_dynamic-update-slice_fusion
  764.3 0.4 convolution_subtract_fusion.1
  764.7 11.7 %cholesky.179 = f32[128,128]{1,0:T(8,128)S(1)} custom-call(f32[128,128]{1,0:T(8,128)S(1)} %convolution_subtract_fusion.1), custom_call_target="Cholesky" | custom-call | tf_op jit(solution)/shard_map/jit(cholesky)/cholesky | solution.py:130
  776.5 0.1 copy.34
  776.6 0.7 compare_reduce_fusion
  777.3 0.6 compare_reduce_fusion.1
  779.9 6.7 while.1
  780.0 0.6 fusion.71
  780.6 1.4 dynamic-slice.8
  782.0 0.1 copy.44
  782.2 0.6 fusion.71
  782.8 1.4 dynamic-slice.8
  784.2 0.1 copy.44
  784.4 0.6 fusion.71
  785.0 1.4 dynamic-slice.8
  786.5 0.1 copy.44
  786.6 29.5 %custom-call.28 = f32[3,128,128]{1,2,0:T(8,128)S(1)} custom-call(f32[3,128,128]{2,1,0:T(8,128)S(1)} %get-tuple-element.9), custom_call_target="InvertDiagBlocksLowerTriangular" | custom-call | tf_op jit(solution)/shard_map/jit(_cho_solve)/triangular_solve | solution.py:131
  816.1 0.2 fusion.25
  816.2 0.2 fusion.5
  816.4 0.2 fusion.26
  816.6 0.2 fusion.6
  816.8 0.2 convolution_bitcast_fusion.5
  816.9 0.2 convolution_bitcast_fusion.4
  817.1 0.2 fusion.2
  817.4 0.2 convolution_bitcast_fusion.2
  817.6 0.2 fusion.7
  817.8 0.2 convolution_bitcast_fusion
  818.0 0.9 fusion.33
  818.9 0.6 multiply_add_fusion.1
  (83 shorter events, 1.8 us)
Async XLA Ops:
  7.2 20.8 %copy-start.11 = (f32[12]{0:T(128)S(1)}, f32[12]{0:T(128)}, u32[]{:S(2)}) copy-start(f32[12]{0:T(128)} %constant.198) | copy-start | bytes 148
  7.2 20.9 %copy-start.10 = (f32[12]{0:T(128)S(1)}, f32[12]{0:T(128)}, u32[]{:S(2)}) copy-start(f32[12]{0:T(128)} %constant.200) | copy-start | bytes 148
  7.2 20.9 %copy-start.9 = (f32[12]{0:T(128)S(1)}, f32[12]{0:T(128)}, u32[]{:S(2)}) copy-start(f32[12]{0:T(128)} %constant.202) | copy-start | bytes 148
  7.2 21.2 %copy-start.3 = (f32[6,3,66]{2,1,0:T(4,128)S(1)}, f32[6,3,66]{2,1,0:T(4,128)}, u32[]{:S(2)}) copy-start(f32[6,3,66]{2,1,0:T(4,128)} %param.14) | copy-start | bytes 14260
  7.2 23.1 %copy-start.4 = (f32[3,21]{1,0:T(4,128)S(1)}, f32[3,21]{1,0:T(4,128)}, u32[]{:S(2)}) copy-start(f32[3,21]{1,0:T(4,128)} %param.15) | copy-start | bytes 760
  7.2 23.2 %copy-start.12 = (s32[21]{0:T(128)S(1)}, s32[21]{0:T(128)}, u32[]{:S(2)}) copy-start(s32[21]{0:T(128)} %param.18) | copy-start | bytes 256
  7.2 23.3 %copy-start.6 = (f32[21,3]{0,1:T(4,128)S(1)}, f32[21,3]{0,1:T(4,128)}, u32[]{:S(2)}) copy-start(f32[21,3]{0,1:T(4,128)} %param.20) | copy-start | bytes 760
  7.2 23.3 %copy-start.7 = (f32[21,3]{0,1:T(4,128)S(1)}, f32[21,3]{0,1:T(4,128)}, u32[]{:S(2)}) copy-start(f32[21,3]{0,1:T(4,128)} %param.19) | copy-start | bytes 760
  7.3 23.3 %copy-start.5 = (s32[6,66]{1,0:T(8,128)S(1)}, s32[6,66]{1,0:T(8,128)}, u32[]{:S(2)}) copy-start(s32[6,66]{1,0:T(8,128)} %param.17) | copy-start | bytes 4756
  7.3 214.3 %all-to-all-start = ((f32[6,64,1024]{2,0,1:T(8,128)}), f32[6,64,1024]{2,0,1:T(8,128)S(1)}, u32[]{:S(2)}, u32[]{:S(2)}) async-start(f32[6,64,1024]{2,0,1:T(8,128)} %bitcast.162), calls=%async_computation | async-start | bytes 4194304 | tf_op jit(solution)/shard_map/all_to_all | solution.py:106
  26.7 4.2 copy-start.1
  26.7 691.5 %all-reduce.4.cloned.1.call-start = ((), (), s32[]{:S(2)}) async-start(), calls=%async_computation.1 | async-start | bytes 1179648 | tf_op jit(solution)/shard_map/psum | solution.py:87
  30.5 1.2 copy-start.8
  225.0 3.5 copy-start.2
  718.2 1.4 copy-start
Sparse Core Ops, SparseCore 0:
  228.5 489.6 all-reduce.3
where the time goes:
time: 827 us; the launch traced here: 826 us
  waiting for transfers between devices  355 us (43%)
  blocking collectives  321 us (39%)
  other arithmetic  92.2 us (11%)
  starting transfers between devices  19.5 us (2%)
  between operations  17.8 us (2%)
  local copies, waits for them, and re-layouts  11.5 us (1%)
  matrix products  9.1 us (1%)
    psum x1, waiting for transfers between devices, sum_pieces(): first_sum, second_sum = lax.psum((first, second), ('walk', 'col'))  355 us
    unnamed x1, blocking collectives  188 us
    psum x1, blocking collectives, sum_pieces(): first_sum, second_sum = lax.psum((first, second), ('walk', 'col'))  133 us
    another operation x10, other arithmetic, body(): factor = jnp.linalg.cholesky(system)  56.4 us
    another operation x3, other arithmetic, body(): solved = jax.scipy.linalg.cho_solve((factor, True), eps - momentum * along)  29.5 us
    all_to_all x1, starting transfers between devices, body(): lax.all_to_all(jacobian, 'walk', split_axis=1, concat_axis=0, tiled=True)  19.4 us
  transfers between devices with their start and end apart: 2, of which 1 were waited for; matrix products, arithmetic and copies ran while one was open for 1% of the time, Pallas kernels for 0%

commit v1 on v0

--- a/solution.py
+++ b/solution.py
@@ -3,6 +3,8 @@
 import jax
 import jax.numpy as jnp
 from jax import lax
+from jax.experimental import pallas as pl
+from jax.experimental.pallas import tpu as pltpu
 from jax.sharding import PartitionSpec as P
 
 NROT = 16
@@ -83,9 +85,94 @@
     return total
 
 
-def sum_pieces(first, second):
-    first_sum, second_sum = lax.psum((first, second), ("walk", "col"))
-    return (first_sum, second_sum)
+BLOCK = 128
+SUB = 8
+LANES = 128
+
+
+def spread_rows(jac_ref, out_ref):
+    rows = jac_ref.shape[0]
+    for tile in range(jac_ref.shape[1] // LANES):
+        owner, sub = divmod(tile, SUB)
+        out_ref[pl.ds(owner * rows * SUB + sub, rows, stride=SUB), :] = jac_ref[
+            :, tile * LANES : (tile + 1) * LANES
+        ]
+
+
+def dense_pieces(jacobian, owners):
+    rows, width = jacobian.shape
+    steps = 8
+    piece = width // owners
+    assert piece == SUB * LANES
+    return pl.pallas_call(
+        spread_rows,
+        grid=(steps,),
+        in_specs=[pl.BlockSpec((rows, width // steps), lambda i: (0, i))],
+        out_specs=pl.BlockSpec((owners // steps * rows * SUB, LANES), lambda i: (i, 0)),
+        out_shape=jax.ShapeDtypeStruct((owners * rows * SUB, LANES), jnp.float32),
+        name="dense_pieces",
+    )(jacobian)
+
+
+def split_high_low(value):
+    high = value.astype(jnp.bfloat16)
+    low = (value - high.astype(jnp.float32)).astype(jnp.bfloat16)
+    return high, low
+
+
+def contract_last(left, right, precision=None):
+    return lax.dot_general(
+        left,
+        right,
+        (((1,), (1,)), ((), ())),
+        precision=precision,
+        preferred_element_type=jnp.float32,
+    )
+
+
+def gram_kernel(scale, x_ref, prev_ref, energy_ref, packed_ref, centred_ref, high_ref, low_ref):
+    walkers = centred_ref.shape[0]
+    for sub in range(SUB):
+        part = x_ref[pl.ds(sub, walkers, stride=SUB), :]
+        part = part - jnp.sum(part, axis=0, keepdims=True) * (1.0 / walkers)
+        lanes = slice(sub * LANES, (sub + 1) * LANES)
+        centred_ref[:, lanes] = part
+        high, low = split_high_low(part)
+        high_ref[:, lanes] = high
+        low_ref[:, lanes] = low
+    blocks = walkers // BLOCK
+    row = 0
+    for i in range(blocks):
+        mine = slice(i * BLOCK, (i + 1) * BLOCK)
+        rest = slice(i * BLOCK, walkers)
+        strip = contract_last(high_ref[mine, :], high_ref[rest, :])
+        strip = strip + contract_last(high_ref[mine, :], low_ref[rest, :])
+        strip = strip + contract_last(low_ref[mine, :], high_ref[rest, :])
+        strip = strip * scale
+        for j in range(blocks - i):
+            packed_ref[row : row + BLOCK, :] = strip[:, j * BLOCK : (j + 1) * BLOCK]
+            row += BLOCK
+    along = contract_last(prev_ref[...], centred_ref[...], lax.Precision.HIGHEST) * scale
+    packed_ref[row:, :] = jnp.zeros((packed_ref.shape[0] - row, LANES), jnp.float32)
+    for j in range(blocks):
+        packed_ref[row + j : row + j + 1, :] = along[:, j * BLOCK : (j + 1) * BLOCK]
+        packed_ref[row + SUB + j : row + SUB + j + 1, :] = energy_ref[:, j * BLOCK : (j + 1) * BLOCK]
+
+
+def gram_pieces(received, prev_update, energy_row, walkers, pieces, scale):
+    width = prev_update.shape[1]
+    return pl.pallas_call(
+        lambda *refs: gram_kernel(scale, *refs),
+        out_shape=(
+            jax.ShapeDtypeStruct((pieces * BLOCK, LANES), jnp.float32),
+            jax.ShapeDtypeStruct((walkers, width), jnp.float32),
+        ),
+        scratch_shapes=[
+            pltpu.VMEM((walkers, width), jnp.bfloat16),
+            pltpu.VMEM((walkers, width), jnp.bfloat16),
+        ],
+        name="gram_pieces",
+    )(received, prev_update, energy_row)
 
 
 def body(
@@ -100,31 +187,47 @@
     ecp_coef,
     ecp_expo,
 ):
+    owners = lax.axis_size("walk")
+    columns = lax.axis_size("col")
+    rows, width = jacobian.shape
+    walkers = rows * owners
+    scale = 1.0 / (width * columns)
+    pieces = dense_pieces(jacobian, owners).reshape(owners, rows * SUB, LANES)
+    received = lax.all_to_all(pieces, "walk", split_axis=0, concat_axis=0, tiled=True)
     energy_mine = base_energy + nonlocal_energy(
         elec_pos, atom_pos, quad_ratio, rotation, channels, ecp_coef, ecp_expo
     )
-    columns = lax.all_to_all(jacobian, "walk", split_axis=1, concat_axis=0, tiled=True)
-    walkers = columns.shape[0]
-    params_total = columns.shape[1] * lax.axis_size("walk") * lax.axis_size("col")
-    scale = 1.0 / params_total
-    centred = columns - jnp.mean(columns, axis=0, keepdims=True)
-    prev_mine = prev_update[0]
-    gram_part = (
-        jnp.dot(
-            centred, centred.T, precision=lax.Precision.HIGHEST, preferred_element_type=jnp.float32
-        )
-        * scale
-    )
-    along_part = (
-        jnp.dot(
-            centred, prev_mine, precision=lax.Precision.HIGHEST, preferred_element_type=jnp.float32
-        )
-        * scale
-    )
-    extra = along_part[:, None]
-    gram, extra_sum = sum_pieces(gram_part, extra)
-    along = extra_sum[:, 0]
-    energies = lax.all_gather(energy_mine, "walk", axis=0, tiled=True)
+    energy_row = lax.dynamic_update_slice(
+        jnp.zeros((walkers,), jnp.float32), energy_mine / columns, (lax.axis_index("walk") * rows,)
+    )
+    packed, centred = gram_pieces(
+        received.reshape(walkers * SUB, LANES),
+        prev_update,
+        energy_row[None, :],
+        walkers,
+        columns,
+        scale,
+    )
+    shares = lax.all_to_all(
+        packed.reshape(columns, BLOCK, LANES), "col", split_axis=0, concat_axis=0, tiled=True
+    )
+    share = jnp.sum(shares, axis=0).reshape(owners, -1, LANES)
+    cells = lax.all_to_all(share, "walk", split_axis=0, concat_axis=0, tiled=True)
+    cell = jnp.sum(cells, axis=0)
+    full = lax.all_to_all(
+        jnp.broadcast_to(cell[None], cells.shape), "walk", split_axis=0, concat_axis=0, tiled=True
+    )
+    whole = lax.all_gather(full.reshape(BLOCK, LANES), "col", axis=0, tiled=False)
+    along = whole[6, 0:3].reshape(walkers)
+    energies = whole[6, SUB : SUB + 3].reshape(walkers)
+    gram = jnp.concatenate(
+        [
+            jnp.concatenate([whole[0], whole[1], whole[2]], axis=1),
+            jnp.concatenate([whole[1].T, whole[3], whole[4]], axis=1),
+            jnp.concatenate([whole[2].T, whole[4].T, whole[5]], axis=1),
+        ],
+        axis=0,
+    )
     eps = -(energies - jnp.mean(energies)) / math.sqrt(walkers)
     system = gram + damping * jnp.eye(walkers, dtype=jnp.float32)
     factor = jnp.linalg.cholesky(system)
@@ -133,7 +236,7 @@
         jnp.dot(
             solved, centred, precision=lax.Precision.HIGHEST, preferred_element_type=jnp.float32
         )
-        + momentum * prev_mine
+        + momentum * prev_update[0]
     )
     return (energy_mine, update_mine[None, :])
 

time: 827 us -> 283 us (0.34)
  waiting for transfers between devices: 355 us -> 83.5 us
  blocking collectives: 321 us -> 55.3 us
  between operations: 17.8 us -> 3.75 us
  Pallas kernels: 0 us -> 10.9 us
    psum x1 -> x0, waiting for transfers between devices: 355 us -> none  [sum_pieces(): first_sum, second_sum = lax.psum((first, second), ('walk', 'col'))]
    unnamed x1 -> x0, blocking collectives: 188 us -> none
    psum x1 -> x0, blocking collectives: 133 us -> none  [sum_pieces(): first_sum, second_sum = lax.psum((first, second), ('walk', 'col'))]
    all_to_all x1 -> x2, waiting for transfers between devices: 0.01 us -> 83.5 us  [the longest x1 69.6 us: body(): lax.all_to_all(pieces, 'walk', split_axis=0, concat_axis=0, tiled=True)]
    all_to_all x0 -> x2, blocking collectives: none -> 38.5 us  [the longest x1 19.5 us: body(): lax.all_to_all(share, 'walk', split_axis=0, concat_axis=0, tiled=True)]
    all_gather x0 -> x1, blocking collectives: none -> 16.8 us  [body(): lax.all_gather(full.reshape(BLOCK, LANES), 'col', axis=0, tiled=False)]
    pallas_call x0 -> x2, Pallas kernels: none -> 10.9 us  [the longest x1 5.63 us: dense_pieces(): pl.pallas_call(spread_rows, grid=(steps,), in_specs=[pl.BlockSpec((rows,...]
    all_to_all x1 -> x2, starting transfers between devices: 19.4 us -> 24 us  [the longest x1 19.4 us: body(): lax.all_to_all(pieces, 'walk', split_axis=0, concat_axis=0, tiled=True)]
  transfers between devices with their start and end apart: 2 -> 2, of which waited for: 1 -> 2; matrix products, arithmetic and copies ran while one was open for 1% -> 1% of each run, Pallas kernels for 0% -> 0%
where the time goes in v1:
time: 283 us; the launch traced here: 282 us
  other arithmetic  90 us (32%)
  waiting for transfers between devices  83.5 us (30%)
  blocking collectives  55.3 us (20%)
  starting transfers between devices  24 us (8%)
  Pallas kernels  10.9 us (4%)
  local copies, waits for them, and re-layouts  10.5 us (4%)
  matrix products  4.25 us (2%)
  between operations  3.75 us (1%)
    all_to_all x1, waiting for transfers between devices, body(): lax.all_to_all(pieces, 'walk', split_axis=0, concat_axis=0, tiled=True)  69.6 us
    another operation x11, other arithmetic, body(): factor = jnp.linalg.cholesky(system)  57 us
    another operation x3, other arithmetic, body(): solved = jax.scipy.linalg.cho_solve((factor, True), eps - momentum * along)  29.5 us
    all_to_all x1, blocking collectives, body(): lax.all_to_all(share, 'walk', split_axis=0, concat_axis=0, tiled=True)  19.5 us
    all_to_all x1, starting transfers between devices, body(): lax.all_to_all(pieces, 'walk', split_axis=0, concat_axis=0, tiled=True)  19.4 us
    all_to_all x1, blocking collectives, body(): lax.all_to_all(packed.reshape(columns, BLOCK, LANES), 'col', split_axis=0...  19 us
    all_gather x1, blocking collectives, body(): lax.all_gather(full.reshape(BLOCK, LANES), 'col', axis=0, tiled=False)  16.8 us
    all_to_all x1, waiting for transfers between devices, body(): lax.all_to_all(jnp.broadcast_to(cell[None], cells.shape), 'walk', split_a...  13.9 us
  transfers between devices with their start and end apart: 2, of which 2 were waited for; matrix products, arithmetic and copies ran while one was open for 1% of the time, Pallas kernels for 0%

profile of v1, /device:TPU:1, one launch (start us, length us, event | category | flops | bytes accessed | tf_op | source)
XLA Modules:
  0.0 282.4 jit_solution(13105249745003773336)
XLA Ops:
  0.6 5.6 %dense_pieces.1 = f32[3072,128]{1,0:T(8,128)} custom-call(f32[6,65536]{1,0:T(8,128)} %jac_ref.1), custom_call_target="tpu_custom_call" | custom-call | tf_op jit(solution)/shard_map/dense_pieces/pallas_call | solution.py:107
  6.3 19.4 %all-to-all-start = ((f32[64,48,128]{2,1,0:T(8,128)}), f32[64,48,128]{2,1,0:T(8,128)S(1)}, u32[]{:S(2)}, u32[]{:S(2)}) async-start(f32[64,48,128]{2,1,0:T(8,128)} %bitcast.183), calls=%async_computation | async-start | bytes 3145728 | tf_op jit(solution)/shard_map/all_to_all | solution.py:196
  27.0 0.1 mul.376
  27.1 0.1 mul.368
  27.3 0.1 copy.84
  27.4 0.1 fusion.13
  27.7 0.2 fusion.28
  27.9 0.1 subtract_divide_fusion
  28.0 0.6 multiply_reduce_fusion
  28.6 0.3 multiply_reduce_fusion.2
  28.8 0.5 multiply_bitcast_fusion
  29.5 69.6 %all-to-all-done = f32[64,48,128]{2,1,0:T(8,128)S(1)} async-done(((f32[64,48,128]{2,1,0:T(8,128)}), f32[64,48,128]{2,1,0:T(8,128)S(1)}, u32[]{:S(2)}, u32[]{:S(2)}) %all-to-all-start) | async-done | bytes 1572896 | tf_op jit(solution)/shard_map/all_to_all | solution.py:196
  99.1 1.1 copy-done
  100.2 5.3 %gram_pieces.1 = (f32[1024,128]{1,0:T(8,128)}, f32[384,1024]{1,0:T(8,128)}) custom-call(f32[3072,128]{1,0:T(8,128)} %bitcast.182, f32[1,1024]{1,0:T(1,128)} %refs_1_.1, f32[1,384]{1,0:T(1,128)} %copy-done.6), custom_call_target="tpu_custom_call" | custom-call | tf_op jit(solution)/shard_map/gram_pieces/pallas_call | solution.py:164
  105.5 19.0 %all_to_all.20 = f32[8,128,128]{2,1,0:T(8,128)S(1)} all-to-all(f32[8,128,128]{2,1,0:T(8,128)} %bitcast.193), channel_id=1, replica_groups=mesh['walk'=64,'col'=8] {'col'}, dimensions={0} | all-to-all | bytes 1048576 | tf_op jit(solution)/shard_map/all_to_all | solution.py:211
  124.6 19.5 %all_to_all.21 = f32[64,2,128]{2,1,0:T(2,128)S(1)} all-to-all(f32[64,2,128]{2,1,0:T(2,128)S(1)} %bitcast.195), channel_id=1, replica_groups=mesh['walk'=64,'col'=8] {'walk'}, dimensions={0} | all-to-all | bytes 131072 | tf_op jit(solution)/shard_map/all_to_all | solution.py:215
  144.1 0.6 broadcast_in_dim.12
  144.8 4.6 %all-to-all-start.3 = ((f32[64,2,128]{2,1,0:T(2,128)}), f32[64,2,128]{2,1,0:T(2,128)S(1)}, u32[]{:S(2)}, u32[]{:S(2)}) async-start(f32[64,2,128]{2,1,0:T(2,128)} %broadcast_in_dim.12), calls=%async_computation.3 | async-start | bytes 131072 | tf_op jit(solution)/shard_map/all_to_all | solution.py:217
  149.4 13.9 %all-to-all-done.3 = f32[64,2,128]{2,1,0:T(2,128)S(1)} async-done(((f32[64,2,128]{2,1,0:T(2,128)}), f32[64,2,128]{2,1,0:T(2,128)S(1)}, u32[]{:S(2)}, u32[]{:S(2)}) %all-to-all-start.3) | async-done | bytes 65568 | tf_op jit(solution)/shard_map/all_to_all | solution.py:217
  163.3 16.8 %all_gather.3 = f32[8,128,128]{2,1,0:T(8,128)S(1)} all-gather(f32[1,128,128]{2,1,0:T(8,128)S(1)} %bitcast.194), channel_id=1, replica_groups=mesh['walk'=64,'col'=8] {'col'}, dimensions={0}, use_global_device_ids=true | all-gather | bytes 589824 | tf_op jit(solution)/shard_map/all_gather | solution.py:220
  180.1 0.6 slice_reduce_fusion
  180.9 0.1 copy.107
  181.0 0.1 copy.91
  181.1 0.1 copy.108
  181.2 0.1 copy.109
  181.4 0.2 copy.92
  181.7 11.7 %cholesky.76 = f32[128,128]{1,0:T(8,128)S(1)} custom-call(f32[128,128]{1,0:T(8,128)S(1)} %cholesky.189), custom_call_target="Cholesky" | custom-call | tf_op jit(solution)/shard_map/jit(cholesky)/cholesky | solution.py:233
  193.4 0.1 copy.93
  193.6 9.8 %custom-call.26 = f32[1,128,128]{1,2,0:T(8,128)S(1)} custom-call(f32[1,128,128]{2,1,0:T(8,128)S(1)} %get-tuple-element.69), custom_call_target="InvertDiagBlocksLowerTriangular" | custom-call | tf_op jit(solution)/shard_map/jit(cholesky)/cholesky | solution.py:233
  203.4 0.3 fusion.17
  203.6 0.3 convolution_subtract_fusion
  203.9 0.1 copy.94
  204.0 11.7 %cholesky.160 = f32[128,128]{1,0:T(8,128)S(1)} custom-call(f32[128,128]{1,0:T(8,128)S(1)} %cholesky.193), custom_call_target="Cholesky" | custom-call | tf_op jit(solution)/shard_map/jit(cholesky)/cholesky | solution.py:233
  215.8 0.1 copy.95
  215.9 10.0 %custom-call.27 = f32[1,128,128]{1,2,0:T(8,128)S(1)} custom-call(f32[1,128,128]{2,1,0:T(8,128)S(1)} %get-tuple-element.67), custom_call_target="InvertDiagBlocksLowerTriangular" | custom-call | tf_op jit(solution)/shard_map/jit(cholesky)/cholesky | solution.py:233
  226.0 0.3 convolution_dynamic-update-slice_fusion
  226.3 0.4 convolution_subtract_fusion.1
  226.7 11.7 %cholesky.179 = f32[128,128]{1,0:T(8,128)S(1)} custom-call(f32[128,128]{1,0:T(8,128)S(1)} %convolution_subtract_fusion.1), custom_call_target="Cholesky" | custom-call | tf_op jit(solution)/shard_map/jit(cholesky)/cholesky | solution.py:233
  238.4 0.1 copy.97
  239.2 0.6 compare_reduce_fusion.2
  239.8 0.7 compare_reduce_fusion.1
  240.5 0.7 compare_reduce_fusion
  243.1 6.3 %while.1 = (s32[]{:T(128)}, f32[384,384]{0,1:T(8,128)S(1)}, s32[3,2]{0,1:T(2,128)S(1)}, f32[3,128,128]{2,1,0:T(8,128)S(1)}, s32[]{:T(128)}) while((s32[]{:T(128)}, f32[384,384]{0,1:T(8,128)S(1)}, s32[3,2]{0,1:T(2,128)S(1)}, f32[3,128,128]{2,1,0:T(8,128)S(1)}, s32[]{:T(128)}) %tuple.59), condition=%wide.while_cond, body=%wide.while_body.sunk | while | flops 2 | bytes 393329 | solution.py:234
  243.2 0.5 fusion.68
  243.8 1.3 dynamic-slice.7
  245.1 0.1 copy.112
  245.3 0.5 fusion.68
  245.9 1.3 dynamic-slice.7
  247.2 0.1 copy.112
  247.4 0.5 fusion.68
  248.0 1.3 dynamic-slice.7
  249.4 29.5 %custom-call.28 = f32[3,128,128]{1,2,0:T(8,128)S(1)} custom-call(f32[3,128,128]{2,1,0:T(8,128)S(1)} %get-tuple-element.13), custom_call_target="InvertDiagBlocksLowerTriangular" | custom-call | tf_op jit(solution)/shard_map/jit(_cho_solve)/triangular_solve | solution.py:234
  278.9 0.2 fusion.25
  279.1 0.2 fusion.5
  279.3 0.2 fusion.26
  279.4 0.2 fusion.6
  279.6 0.2 convolution_bitcast_fusion.5
  279.8 0.2 convolution_bitcast_fusion.4
  280.0 0.2 fusion.2
  280.2 0.2 convolution_bitcast_fusion.2
  280.4 0.2 fusion.7
  280.7 0.2 convolution_bitcast_fusion
  280.9 0.9 fusion.33
  281.8 0.6 add.90
  (92 shorter events, 2.5 us)
Async XLA Ops:
  6.3 19.5 %copy-start.12 = (f32[12]{0:T(128)S(1)}, f32[12]{0:T(128)}, u32[]{:S(2)}) copy-start(f32[12]{0:T(128)} %constant.209) | copy-start | bytes 148
  6.3 19.6 %copy-start.11 = (f32[12]{0:T(128)S(1)}, f32[12]{0:T(128)}, u32[]{:S(2)}) copy-start(f32[12]{0:T(128)} %constant.211) | copy-start | bytes 148
  6.3 19.7 %copy-start.10 = (f32[12]{0:T(128)S(1)}, f32[12]{0:T(128)}, u32[]{:S(2)}) copy-start(f32[12]{0:T(128)} %constant.213) | copy-start | bytes 148
  6.3 20.5 %copy-start.4 = (f32[6,3,66]{2,1,0:T(4,128)S(1)}, f32[6,3,66]{2,1,0:T(4,128)}, u32[]{:S(2)}) copy-start(f32[6,3,66]{2,1,0:T(4,128)} %param.14) | copy-start | bytes 14260
  6.3 21.2 %copy-start.5 = (f32[3,21]{1,0:T(4,128)S(1)}, f32[3,21]{1,0:T(4,128)}, u32[]{:S(2)}) copy-start(f32[3,21]{1,0:T(4,128)} %param.15) | copy-start | bytes 760
  6.3 21.3 %copy-start.14 = (s32[21]{0:T(128)S(1)}, s32[21]{0:T(128)}, u32[]{:S(2)}) copy-start(s32[21]{0:T(128)} %param.18) | copy-start | bytes 256
  6.3 21.3 %copy-start.8 = (f32[21,3]{0,1:T(4,128)S(1)}, f32[21,3]{0,1:T(4,128)}, u32[]{:S(2)}) copy-start(f32[21,3]{0,1:T(4,128)} %param.20) | copy-start | bytes 760
  6.3 21.3 %copy-start.9 = (f32[21,3]{0,1:T(4,128)S(1)}, f32[21,3]{0,1:T(4,128)}, u32[]{:S(2)}) copy-start(f32[21,3]{0,1:T(4,128)} %param.19) | copy-start | bytes 760
  6.3 21.3 %copy-start.7 = (s32[6,66]{1,0:T(8,128)S(1)}, s32[6,66]{1,0:T(8,128)}, u32[]{:S(2)}) copy-start(s32[6,66]{1,0:T(8,128)} %param.17) | copy-start | bytes 4756
  6.3 92.8 %all-to-all-start = ((f32[64,48,128]{2,1,0:T(8,128)}), f32[64,48,128]{2,1,0:T(8,128)S(1)}, u32[]{:S(2)}, u32[]{:S(2)}) async-start(f32[64,48,128]{2,1,0:T(8,128)} %bitcast.183), calls=%async_computation | async-start | bytes 3145728 | tf_op jit(solution)/shard_map/all_to_all | solution.py:196
  25.8 2.2 copy-start.2
  27.6 1.2 copy-start.13
  29.5 69.6 %copy-start.6 = (f32[1,384]{1,0:T(1,128)}, f32[1,384]{1,0:T(1,128)S(1)}, u32[]{:S(2)}) copy-start(f32[1,384]{1,0:T(1,128)S(1)} %dynamic_update_slice.4.refs_2_) | copy-start | bytes 4612
  99.1 1.1 copy-start
  100.2 49.2 %copy-start.3 = (f32[1,1024]{1,0:T(1,128)S(1)}, f32[1,1024]{1,0:T(1,128)}, u32[]{:S(2)}) copy-start(f32[1,1024]{1,0:T(1,128)} %refs_1_.1) | copy-start | bytes 12292
  144.8 18.6 %all-to-all-start.3 = ((f32[64,2,128]{2,1,0:T(2,128)}), f32[64,2,128]{2,1,0:T(2,128)S(1)}, u32[]{:S(2)}, u32[]{:S(2)}) async-start(f32[64,2,128]{2,1,0:T(2,128)} %broadcast_in_dim.12), calls=%async_computation.3 | async-start | bytes 131072 | tf_op jit(solution)/shard_map/all_to_all | solution.py:217
  243.1 37.8 %copy-start.1 = (f32[384,1024]{1,0:T(8,128)S(1)}, f32[384,1024]{1,0:T(8,128)}, u32[]{:S(2)}) copy-start(f32[384,1024]{1,0:T(8,128)} %get-tuple-element.5) | copy-start | bytes 4718596

commit v2 on v1

--- a/solution.py
+++ b/solution.py
@@ -163,6 +163,8 @@
     width = prev_update.shape[1]
     return pl.pallas_call(
         lambda *refs: gram_kernel(scale, *refs),
+        in_specs=[pl.BlockSpec(memory_space=pltpu.VMEM)] * 3,
+        out_specs=[pl.BlockSpec(memory_space=pltpu.VMEM)] * 2,
         out_shape=(
             jax.ShapeDtypeStruct((pieces * BLOCK, LANES), jnp.float32),
             jax.ShapeDtypeStruct((walkers, width), jnp.float32),
@@ -173,6 +175,96 @@
         ],
         name="gram_pieces",
     )(received, prev_update, energy_row)
+
+
+def matmul(left, right, left_dim=1, right_dim=0):
+    return lax.dot_general(
+        left,
+        right,
+        (((left_dim,), (right_dim,)), ((), ())),
+        precision=lax.Precision.HIGHEST,
+        preferred_element_type=jnp.float32,
+    )
+
+
+def inverse(block):
+    lane = lax.broadcasted_iota(jnp.int32, (SUB, BLOCK), 1)
+    row_of = lax.broadcasted_iota(jnp.int32, (SUB, BLOCK), 0)
+    lane_rest = lax.broadcasted_iota(jnp.int32, (BLOCK - SUB, BLOCK), 1)
+    full = (SUB, BLOCK)
+
+    def step(_, value):
+        panel, rest = value[:SUB], value[SUB:]
+        columns = [rest[:, k : k + 1] for k in range(SUB)]
+        pivots = [jnp.broadcast_to(panel[:, k : k + 1], full) for k in range(SUB)]
+        for k in range(SUB):
+            column = pivots[k]
+            scale = 1.0 / jnp.broadcast_to(column[k : k + 1, :], full)
+            mine = row_of == k
+            row = jnp.broadcast_to(panel[k : k + 1, :], full)
+            row = jnp.where(lane == k, scale, row * scale)
+            panel = jnp.where(mine, row, jnp.where(lane == k, 0.0, panel) - column * row)
+            for j in range(k + 1, SUB):
+                other = jnp.broadcast_to(pivots[j][k : k + 1, :], full) * scale
+                pivots[j] = jnp.where(mine, other, pivots[j] - column * other)
+        rest = jnp.where(lane_rest < SUB, 0.0, rest)
+        for k in range(SUB):
+            rest = rest - columns[k] * panel[k : k + 1, :]
+        return pltpu.roll(jnp.concatenate([rest, panel], axis=0), BLOCK - SUB, 1)
+
+    return lax.fori_loop(0, BLOCK // SUB, step, block)
+
+
+def solve_kernel(whole_ref, centred_ref, prev_ref, out_ref):
+    lane = lax.broadcasted_iota(jnp.int32, (BLOCK, BLOCK), 1)
+    row_of = lax.broadcasted_iota(jnp.int32, (BLOCK, BLOCK), 0)
+    shift = jnp.where(lane == row_of, damping, 0.0)
+    walkers = centred_ref.shape[0]
+
+    def gram(index):
+        return whole_ref[index * BLOCK : (index + 1) * BLOCK, :]
+
+    along = [whole_ref[6 * BLOCK + j : 6 * BLOCK + j + 1, :] for j in range(3)]
+    energies = [whole_ref[6 * BLOCK + SUB + j : 6 * BLOCK + SUB + j + 1, :] for j in range(3)]
+    mean = sum(jnp.sum(part, axis=1, keepdims=True) for part in energies) * (1.0 / walkers)
+    right = [
+        (mean - energy) * (1.0 / math.sqrt(walkers)) - momentum * part
+        for energy, part in zip(energies, along)
+    ]
+    g01, g02, g12 = gram(1), gram(2), gram(4)
+    inv0 = inverse(gram(0) + shift)
+    w01, w02 = matmul(inv0, g01), matmul(inv0, g02)
+    s11 = gram(3) + shift - matmul(g01, w01, 0, 0)
+    s12 = g12 - matmul(g01, w02, 0, 0)
+    s22 = gram(5) + shift - matmul(g02, w02, 0, 0)
+    y0 = matmul(right[0], inv0)
+    r1 = right[1] - matmul(y0, g01)
+    r2 = right[2] - matmul(y0, g02)
+    inv1 = inverse(s11)
+    w12 = matmul(inv1, s12)
+    s22 = s22 - matmul(s12, w12, 0, 0)
+    y1 = matmul(r1, inv1)
+    r2 = r2 - matmul(y1, s12)
+    inv2 = inverse(s22)
+    x2 = matmul(r2, inv2)
+    x1 = y1 - matmul(x2, w12, 1, 1)
+    x0 = y0 - matmul(x1, w01, 1, 1) - matmul(x2, w02, 1, 1)
+    out_ref[...] = (
+        matmul(x0, centred_ref[0:BLOCK, :])
+        + matmul(x1, centred_ref[BLOCK : 2 * BLOCK, :])
+        + matmul(x2, centred_ref[2 * BLOCK :, :])
+        + momentum * prev_ref[...]
+    )
+
+
+def solve_update(whole, centred, prev_update):
+    return pl.pallas_call(
+        solve_kernel,
+        in_specs=[pl.BlockSpec(memory_space=pltpu.VMEM)] * 3,
+        out_specs=pl.BlockSpec(memory_space=pltpu.VMEM),
+        out_shape=jax.ShapeDtypeStruct(prev_update.shape, jnp.float32),
+        name="solve_update",
+    )(whole, centred, prev_update)
 
 
 def body(
@@ -218,27 +310,8 @@
         jnp.broadcast_to(cell[None], cells.shape), "walk", split_axis=0, concat_axis=0, tiled=True
     )
     whole = lax.all_gather(full.reshape(BLOCK, LANES), "col", axis=0, tiled=False)
-    along = whole[6, 0:3].reshape(walkers)
-    energies = whole[6, SUB : SUB + 3].reshape(walkers)
-    gram = jnp.concatenate(
-        [
-            jnp.concatenate([whole[0], whole[1], whole[2]], axis=1),
-            jnp.concatenate([whole[1].T, whole[3], whole[4]], axis=1),
-            jnp.concatenate([whole[2].T, whole[4].T, whole[5]], axis=1),
-        ],
-        axis=0,
-    )
-    eps = -(energies - jnp.mean(energies)) / math.sqrt(walkers)
-    system = gram + damping * jnp.eye(walkers, dtype=jnp.float32)
-    factor = jnp.linalg.cholesky(system)
-    solved = jax.scipy.linalg.cho_solve((factor, True), eps - momentum * along)
-    update_mine = (
-        jnp.dot(
-            solved, centred, precision=lax.Precision.HIGHEST, preferred_element_type=jnp.float32
-        )
-        + momentum * prev_update[0]
-    )
-    return (energy_mine, update_mine[None, :])
+    update_mine = solve_update(whole.reshape(columns * BLOCK, LANES), centred, prev_update)
+    return (energy_mine, update_mine)
 
 
 def solution(mesh):

time: 283 us -> 200 us (0.71)
  other arithmetic: 90 us -> 2.06 us
  Pallas kernels: 10.9 us -> 31 us
  blocking collectives: 55.3 us -> 74 us
  waiting for transfers between devices: 83.5 us -> 69.6 us
  local copies, waits for them, and re-layouts: 10.5 us -> 2.53 us
  starting transfers between devices: 24 us -> 19.4 us
  matrix products: 4.25 us -> 0.2 us
  between operations: 3.75 us -> 0.92 us
    another operation x14 -> x0, other arithmetic: 86.6 us -> none  [the longest x11 57 us: body(): factor = jnp.linalg.cholesky(system)]
    pallas_call x1 -> x2, Pallas kernels: 5.27 us -> 25.4 us  [the longest x1 20.1 us: solve_update(): pl.pallas_call(solve_kernel, in_specs=[pl.BlockSpec(memory_space=pltpu.VM...]
    all_to_all x0 -> x1, blocking collectives: none -> 17.8 us  [body(): lax.all_to_all(jnp.broadcast_to(cell[None], cells.shape), 'walk', split_a...]
    all_to_all x1 -> x0, waiting for transfers between devices: 13.9 us -> none  [body(): lax.all_to_all(jnp.broadcast_to(cell[None], cells.shape), 'walk', split_a...]
    another operation x26 -> x0, local copies, waits for them, and re-layouts: 6.64 us -> none
    all_to_all x1 -> x0, starting transfers between devices: 4.6 us -> none  [body(): lax.all_to_all(jnp.broadcast_to(cell[None], cells.shape), 'walk', split_a...]
    another operation x14 -> x0, matrix products: 3.15 us -> none  [the longest x10 1.94 us: body(): solved = jax.scipy.linalg.cho_solve((factor, True), eps - momentum * along)]
  transfers between devices with their start and end apart: 2 -> 1, of which waited for: 2 -> 1; matrix products, arithmetic and copies ran while one was open for 1% -> 2% of each run, Pallas kernels for 0% -> 0%
where the time goes in v2:
time: 200 us
  blocking collectives  74 us (37%)
  waiting for transfers between devices  69.6 us (35%)
  Pallas kernels  31 us (16%)
  starting transfers between devices  19.4 us (10%)
  local copies, waits for them, and re-layouts  2.53 us (1%)
  other arithmetic  2.06 us (1%)
    all_to_all x1, waiting for transfers between devices, body(): lax.all_to_all(pieces, 'walk', split_axis=0, concat_axis=0, tiled=True)  69.6 us
    pallas_call x1, Pallas kernels, solve_update(): pl.pallas_call(solve_kernel, in_specs=[pl.BlockSpec(memory_space=pltpu.VM...  20.1 us
    all_to_all x1, blocking collectives, body(): lax.all_to_all(share, 'walk', split_axis=0, concat_axis=0, tiled=True)  19.5 us
    all_to_all x1, starting transfers between devices, body(): lax.all_to_all(pieces, 'walk', split_axis=0, concat_axis=0, tiled=True)  19.4 us
    all_to_all x1, blocking collectives, body(): lax.all_to_all(packed.reshape(columns, BLOCK, LANES), 'col', split_axis=0...  19.1 us
    all_to_all x1, blocking collectives, body(): lax.all_to_all(jnp.broadcast_to(cell[None], cells.shape), 'walk', split_a...  17.8 us
    all_gather x1, blocking collectives, body(): lax.all_gather(full.reshape(BLOCK, LANES), 'col', axis=0, tiled=False)  17.7 us
    pallas_call x1, Pallas kernels, dense_pieces(): pl.pallas_call(spread_rows, grid=(steps,), in_specs=[pl.BlockSpec((rows,...  5.65 us
  transfers between devices with their start and end apart: 1, of which 1 were waited for; matrix products, arithmetic and copies ran while one was open for 2% of the time, Pallas kernels for 0%

profile of v2, /device:TPU:1, one launch (start us, length us, event | category | flops | bytes accessed | tf_op | source)
XLA Modules:
  0.0 199.8 jit_solution(8044515829472626948)
XLA Ops:
  0.6 5.7 %dense_pieces.1 = f32[3072,128]{1,0:T(8,128)} custom-call(f32[6,65536]{1,0:T(8,128)} %jac_ref.1), custom_call_target="tpu_custom_call" | custom-call | tf_op jit(solution)/shard_map/dense_pieces/pallas_call | solution.py:107
  6.3 0.0 copy-start.10
  6.3 0.0 copy-start.9
  6.3 0.0 copy-start.8
  6.3 0.0 copy-start.2
  6.3 0.0 copy-start.3
  6.3 0.0 copy-start.12
  6.3 0.0 copy-start.6
  6.3 0.0 copy-start.7
  6.3 0.0 copy-start.5
  6.4 19.4 %all-to-all-start = ((f32[64,48,128]{2,1,0:T(8,128)}), f32[64,48,128]{2,1,0:T(8,128)S(1)}, u32[]{:S(2)}, u32[]{:S(2)}) async-start(f32[64,48,128]{2,1,0:T(8,128)} %bitcast.55), calls=%async_computation | async-start | bytes 3145728 | tf_op jit(solution)/shard_map/all_to_all | solution.py:288
  25.8 0.0 copy-start.1
  25.8 0.0 copy-done.10
  25.8 0.1 mul.349
  25.9 0.0 copy-done.9
  25.9 0.1 mul.357
  26.0 0.0 copy-done.8
  26.0 0.1 mul.365
  26.1 0.1 fusion.15
  26.2 0.1 fusion.14
  26.2 0.1 negate_multiply_fusion.1
  26.3 0.1 negate_multiply_fusion
  26.4 0.1 maximum_bitcast_fusion.2
  26.5 0.1 copy.36
  26.6 0.1 copy.37
  26.7 0.1 copy.38
  26.8 0.0 copy-done.2
  26.8 0.1 mul.361
  26.8 0.1 mul.362
  26.9 0.1 mul.353
  27.0 0.1 mul.354
  27.1 0.1 mul.345
  27.2 0.1 mul.346
  27.3 0.1 dot_general.8
  27.3 0.1 copy.33
  27.4 0.0 copy-done.3
  27.4 0.1 fusion.4
  27.6 0.0 copy-done.12
  27.6 0.0 copy-done.6
  27.6 0.0 copy-done.7
  27.6 0.0 copy-start.11
  27.7 0.0 copy-done.5
  27.7 0.2 fusion.6
  27.9 0.1 subtract_divide_fusion
  28.0 0.0 copy-done.1
  28.0 0.6 multiply_reduce_fusion
  28.6 0.3 multiply_reduce_fusion.2
  28.9 0.0 copy-done.11
  28.9 0.5 multiply_bitcast_fusion
  29.4 0.1 dynamic_update_slice.4.refs_2_
  29.5 0.0 copy-start.4
  29.5 69.6 %all-to-all-done = f32[64,48,128]{2,1,0:T(8,128)S(1)} async-done(((f32[64,48,128]{2,1,0:T(8,128)}), f32[64,48,128]{2,1,0:T(8,128)S(1)}, u32[]{:S(2)}, u32[]{:S(2)}) %all-to-all-start) | async-done | bytes 1572896 | tf_op jit(solution)/shard_map/all_to_all | solution.py:288
  99.1 0.0 copy-start
  99.1 0.0 copy-done.4
  99.1 1.1 copy-done
  100.3 5.3 %gram_pieces.1 = (f32[1024,128]{1,0:T(8,128)}, f32[384,1024]{1,0:T(8,128)}) custom-call(f32[3072,128]{1,0:T(8,128)} %bitcast.54, f32[1,1024]{1,0:T(1,128)} %prev_ref.1, f32[1,384]{1,0:T(1,128)} %copy-done.4), custom_call_target="tpu_custom_call" | custom-call | tf_op jit(solution)/shard_map/gram_pieces/pallas_call | solution.py:164
  105.5 19.1 %all_to_all.20 = f32[8,128,128]{2,1,0:T(8,128)S(1)} all-to-all(f32[8,128,128]{2,1,0:T(8,128)} %bitcast.57), channel_id=1, replica_groups=mesh['walk'=64,'col'=8] {'col'}, dimensions={0} | all-to-all | bytes 1048576 | tf_op jit(solution)/shard_map/all_to_all | solution.py:303
  124.6 19.5 %all_to_all.21 = f32[64,2,128]{2,1,0:T(2,128)S(1)} all-to-all(f32[64,2,128]{2,1,0:T(2,128)S(1)} %bitcast.59), channel_id=1, replica_groups=mesh['walk'=64,'col'=8] {'walk'}, dimensions={0} | all-to-all | bytes 131072 | tf_op jit(solution)/shard_map/all_to_all | solution.py:307
  144.1 0.1 reduce_sum.89
  144.2 17.8 %all_to_all.22 = f32[64,2,128]{2,1,0:T(2,128)S(1)} all-to-all(f32[64,2,128]{2,1,0:T(2,128)S(1)} %broadcast_in_dim.8), channel_id=1, replica_groups=mesh['walk'=64,'col'=8] {'walk'}, dimensions={0} | all-to-all | bytes 131072 | tf_op jit(solution)/shard_map/all_to_all | solution.py:309
  162.0 17.7 %all_gather.3 = f32[8,128,128]{2,1,0:T(8,128)} all-gather(f32[1,128,128]{2,1,0:T(8,128)S(1)} %bitcast.58), channel_id=1, replica_groups=mesh['walk'=64,'col'=8] {'col'}, dimensions={0}, use_global_device_ids=true | all-gather | bytes 589824 | tf_op jit(solution)/shard_map/all_gather | solution.py:312
  179.6 20.1 %solve_update.1 = f32[1,1024]{1,0:T(1,128)} custom-call(f32[1024,128]{1,0:T(8,128)} %bitcast.56, f32[384,1024]{1,0:T(8,128)} %get-tuple-element.5.centred_ref, f32[1,1024]{1,0:T(1,128)} %prev_ref.1), custom_call_target="tpu_custom_call" | custom-call | tf_op jit(solution)/shard_map/solve_update/pallas_call | solution.py:261
  (19 shorter events, 0.2 us)
Async XLA Ops:
  6.3 19.5 %copy-start.10 = (f32[12]{0:T(128)S(1)}, f32[12]{0:T(128)}, u32[]{:S(2)}) copy-start(f32[12]{0:T(128)} %constant.63) | copy-start | bytes 148
  6.3 19.6 %copy-start.9 = (f32[12]{0:T(128)S(1)}, f32[12]{0:T(128)}, u32[]{:S(2)}) copy-start(f32[12]{0:T(128)} %constant.65) | copy-start | bytes 148
  6.3 19.7 %copy-start.8 = (f32[12]{0:T(128)S(1)}, f32[12]{0:T(128)}, u32[]{:S(2)}) copy-start(f32[12]{0:T(128)} %constant.67) | copy-start | bytes 148
  6.3 20.5 %copy-start.2 = (f32[6,3,66]{2,1,0:T(4,128)S(1)}, f32[6,3,66]{2,1,0:T(4,128)}, u32[]{:S(2)}) copy-start(f32[6,3,66]{2,1,0:T(4,128)} %param.14) | copy-start | bytes 14260
  6.3 21.2 %copy-start.3 = (f32[3,21]{1,0:T(4,128)S(1)}, f32[3,21]{1,0:T(4,128)}, u32[]{:S(2)}) copy-start(f32[3,21]{1,0:T(4,128)} %param.15) | copy-start | bytes 760
  6.3 21.3 %copy-start.12 = (s32[21]{0:T(128)S(1)}, s32[21]{0:T(128)}, u32[]{:S(2)}) copy-start(s32[21]{0:T(128)} %param.18) | copy-start | bytes 256
  6.3 21.3 %copy-start.6 = (f32[21,3]{0,1:T(4,128)S(1)}, f32[21,3]{0,1:T(4,128)}, u32[]{:S(2)}) copy-start(f32[21,3]{0,1:T(4,128)} %param.20) | copy-start | bytes 760
  6.3 21.3 %copy-start.7 = (f32[21,3]{0,1:T(4,128)S(1)}, f32[21,3]{0,1:T(4,128)}, u32[]{:S(2)}) copy-start(f32[21,3]{0,1:T(4,128)} %param.19) | copy-start | bytes 760
  6.3 21.3 %copy-start.5 = (s32[6,66]{1,0:T(8,128)S(1)}, s32[6,66]{1,0:T(8,128)}, u32[]{:S(2)}) copy-start(s32[6,66]{1,0:T(8,128)} %param.17) | copy-start | bytes 4756
  6.4 92.8 %all-to-all-start = ((f32[64,48,128]{2,1,0:T(8,128)}), f32[64,48,128]{2,1,0:T(8,128)S(1)}, u32[]{:S(2)}, u32[]{:S(2)}) async-start(f32[64,48,128]{2,1,0:T(8,128)} %bitcast.55), calls=%async_computation | async-start | bytes 3145728 | tf_op jit(solution)/shard_map/all_to_all | solution.py:288
  25.8 2.2 %copy-start.1 = (f32[6,21,66,12]{2,1,3,0:T(8,128)S(1)}, f32[6,21,66,12]{2,1,3,0:T(8,128)}, u32[]{:S(2)}) copy-start(f32[6,21,66,12]{2,1,3,0:T(8,128)} %param.16) | copy-start | bytes 1197508
  27.6 1.2 copy-start.11
  29.5 69.6 %copy-start.4 = (f32[1,384]{1,0:T(1,128)}, f32[1,384]{1,0:T(1,128)S(1)}, u32[]{:S(2)}) copy-start(f32[1,384]{1,0:T(1,128)S(1)} %dynamic_update_slice.4.refs_2_) | copy-start | bytes 4612
  99.1 1.2 copy-start

commit v3 on v2

--- a/solution.py
+++ b/solution.py
@@ -86,8 +86,12 @@
 
 
 BLOCK = 128
+HALF = 64
 SUB = 8
 LANES = 128
+WALK = ("z", "y")
+COL = ("x", "core")
+PLANE = ("core", "x", "y")
 
 
 def spread_rows(jac_ref, out_ref):
@@ -101,7 +105,7 @@
 
 def dense_pieces(jacobian, owners):
     rows, width = jacobian.shape
-    steps = 8
+    steps = 2
     piece = width // owners
     assert piece == SUB * LANES
     return pl.pallas_call(
@@ -153,21 +157,23 @@
             packed_ref[row : row + BLOCK, :] = strip[:, j * BLOCK : (j + 1) * BLOCK]
             row += BLOCK
     along = contract_last(prev_ref[...], centred_ref[...], lax.Precision.HIGHEST) * scale
-    packed_ref[row:, :] = jnp.zeros((packed_ref.shape[0] - row, LANES), jnp.float32)
-    for j in range(blocks):
-        packed_ref[row + j : row + j + 1, :] = along[:, j * BLOCK : (j + 1) * BLOCK]
-        packed_ref[row + SUB + j : row + SUB + j + 1, :] = energy_ref[:, j * BLOCK : (j + 1) * BLOCK]
-
-
-def gram_pieces(received, prev_update, energy_row, walkers, pieces, scale):
+    for j in range(walkers // HALF):
+        part = slice(j * HALF, (j + 1) * HALF)
+        packed_ref[HALF + j : HALF + j + 1, :HALF] = along[:, part]
+        packed_ref[HALF + SUB + j : HALF + SUB + j + 1, :HALF] = energy_ref[:, part]
+
+
+def gram_pieces(received, prev_update, energy_row, walkers, scale):
     width = prev_update.shape[1]
+    blocks = walkers // BLOCK
+    pieces = blocks * (blocks + 1) // 2
     return pl.pallas_call(
         lambda *refs: gram_kernel(scale, *refs),
         in_specs=[pl.BlockSpec(memory_space=pltpu.VMEM)] * 3,
         out_specs=[pl.BlockSpec(memory_space=pltpu.VMEM)] * 2,
         out_shape=(
-            jax.ShapeDtypeStruct((pieces * BLOCK, LANES), jnp.float32),
-            jax.ShapeDtypeStruct((walkers, width), jnp.float32),
+            pltpu.VMEM((pieces * BLOCK, LANES), jnp.float32),
+            pltpu.VMEM((walkers, width), jnp.float32),
         ),
         scratch_shapes=[
             pltpu.VMEM((walkers, width), jnp.bfloat16),
@@ -175,6 +181,10 @@
         ],
         name="gram_pieces",
     )(received, prev_update, energy_row)
+
+
+def near(value):
+    return pltpu.with_memory_space_constraint(value, pltpu.VMEM)
 
 
 def matmul(left, right, left_dim=1, right_dim=0):
@@ -224,15 +234,22 @@
     def gram(index):
         return whole_ref[index * BLOCK : (index + 1) * BLOCK, :]
 
-    along = [whole_ref[6 * BLOCK + j : 6 * BLOCK + j + 1, :] for j in range(3)]
-    energies = [whole_ref[6 * BLOCK + SUB + j : 6 * BLOCK + SUB + j + 1, :] for j in range(3)]
+    def vector(first):
+        halves = [whole_ref[first + j : first + j + 1, :HALF] for j in range(walkers // HALF)]
+        return [jnp.concatenate(halves[j : j + 2], axis=1) for j in range(0, len(halves), 2)]
+
+    along = vector(HALF)
+    energies = vector(HALF + SUB)
+    corner = whole_ref[:HALF, HALF:BLOCK].T
+    lower = jnp.concatenate([corner, whole_ref[HALF:BLOCK, HALF:BLOCK]], axis=1)
+    g00 = jnp.concatenate([whole_ref[:HALF, :], lower], axis=0)
     mean = sum(jnp.sum(part, axis=1, keepdims=True) for part in energies) * (1.0 / walkers)
     right = [
         (mean - energy) * (1.0 / math.sqrt(walkers)) - momentum * part
         for energy, part in zip(energies, along)
     ]
     g01, g02, g12 = gram(1), gram(2), gram(4)
-    inv0 = inverse(gram(0) + shift)
+    inv0 = inverse(g00 + shift)
     w01, w02 = matmul(inv0, g01), matmul(inv0, g02)
     s11 = gram(3) + shift - matmul(g01, w01, 0, 0)
     s12 = g12 - matmul(g01, w02, 0, 0)
@@ -267,6 +284,14 @@
     )(whole, centred, prev_update)
 
 
+def exchange(pieces, axes):
+    return lax.all_to_all(pieces, axes, split_axis=0, concat_axis=0, tiled=True)
+
+
+def hand_round(value, axes):
+    return exchange(jnp.broadcast_to(value[None], (lax.axis_size(axes), *value.shape)), axes)
+
+
 def body(
     jacobian,
     prev_update,
@@ -279,53 +304,46 @@
     ecp_coef,
     ecp_expo,
 ):
-    owners = lax.axis_size("walk")
-    columns = lax.axis_size("col")
+    owners = lax.axis_size(WALK)
+    columns = lax.axis_size(COL)
     rows, width = jacobian.shape
     walkers = rows * owners
     scale = 1.0 / (width * columns)
-    pieces = dense_pieces(jacobian, owners).reshape(owners, rows * SUB, LANES)
-    received = lax.all_to_all(pieces, "walk", split_axis=0, concat_axis=0, tiled=True)
     energy_mine = base_energy + nonlocal_energy(
         elec_pos, atom_pos, quad_ratio, rotation, channels, ecp_coef, ecp_expo
     )
     energy_row = lax.dynamic_update_slice(
-        jnp.zeros((walkers,), jnp.float32), energy_mine / columns, (lax.axis_index("walk") * rows,)
-    )
+        jnp.zeros((1, walkers), jnp.float32),
+        energy_mine[None, :] / columns,
+        (0, lax.axis_index(WALK) * rows),
+    )
+    pieces = dense_pieces(jacobian, owners).reshape(owners, rows * SUB, LANES)
+    pieces, energy_row = lax.optimization_barrier((pieces, energy_row))
+    received = exchange(pieces, WALK)
     packed, centred = gram_pieces(
-        received.reshape(walkers * SUB, LANES),
-        prev_update,
-        energy_row[None, :],
-        walkers,
-        columns,
-        scale,
-    )
-    shares = lax.all_to_all(
-        packed.reshape(columns, BLOCK, LANES), "col", split_axis=0, concat_axis=0, tiled=True
-    )
-    share = jnp.sum(shares, axis=0).reshape(owners, -1, LANES)
-    cells = lax.all_to_all(share, "walk", split_axis=0, concat_axis=0, tiled=True)
-    cell = jnp.sum(cells, axis=0)
-    full = lax.all_to_all(
-        jnp.broadcast_to(cell[None], cells.shape), "walk", split_axis=0, concat_axis=0, tiled=True
-    )
-    whole = lax.all_gather(full.reshape(BLOCK, LANES), "col", axis=0, tiled=False)
-    update_mine = solve_update(whole.reshape(columns * BLOCK, LANES), centred, prev_update)
+        near(received.reshape(walkers * SUB, LANES)), prev_update, near(energy_row), walkers, scale
+    )
+    plane = lax.axis_size(PLANE)
+    share = jnp.sum(exchange(packed.reshape(plane, -1, LANES), PLANE), axis=0)
+    share = jnp.sum(hand_round(share, "z"), axis=0)
+    whole = hand_round(share, PLANE)
+    update_mine = solve_update(near(whole.reshape(packed.shape)), near(centred), prev_update)
     return (energy_mine, update_mine)
 
 
 def solution(mesh):
+    mesh = jax.sharding.Mesh(mesh.devices.reshape(16, 4, 4, 2), ("z", "y", "x", "core"))
     in_specs = (
-        P("walk", "col"),
-        P("col", "walk"),
-        P("walk"),
-        P("walk", None, None),
+        P(WALK, COL),
+        P(COL, WALK),
+        P(WALK),
+        P(WALK, None, None),
         P(),
-        P("walk", None, None, None),
-        P("walk", None),
+        P(WALK, None, None, None),
+        P(WALK, None),
         P(),
         P(),
         P(),
     )
-    out_specs = (P("walk"), P("col", "walk"))
+    out_specs = (P(WALK), P(COL, WALK))
     return jax.shard_map(body, mesh=mesh, in_specs=in_specs, out_specs=out_specs, check_vma=False)

time: 200 us -> 184 us (0.920)
  blocking collectives: 74 us -> 147 us
  waiting for transfers between devices: 69.6 us -> 0 us
  starting transfers between devices: 19.4 us -> 0 us
  Pallas kernels: 31 us -> 25.9 us
  other arithmetic: 2.06 us -> 4.69 us
    all_to_all x3 -> x4, blocking collectives: 56.3 us -> 147 us  [exchange(): return lax.all_to_all(pieces, axes, split_axis=0, concat_axis=0, tiled=True)]
    all_to_all x1 -> x0, waiting for transfers between devices: 69.6 us -> none  [body(): lax.all_to_all(pieces, 'walk', split_axis=0, concat_axis=0, tiled=True)]
    all_to_all x1 -> x0, starting transfers between devices: 19.4 us -> none  [body(): lax.all_to_all(pieces, 'walk', split_axis=0, concat_axis=0, tiled=True)]
    all_gather x1 -> x0, blocking collectives: 17.7 us -> none  [body(): lax.all_gather(full.reshape(BLOCK, LANES), 'col', axis=0, tiled=False)]
    pallas_call x1, Pallas kernels: 5.65 us -> 2.71 us  [dense_pieces(): pl.pallas_call(spread_rows, grid=(steps,), in_specs=[pl.BlockSpec((rows,...]
  transfers between devices with their start and end apart: 1 -> 0, of which waited for: 1 -> 0; matrix products, arithmetic and copies ran while one was open for 2% -> 0% of each run, Pallas kernels for 0% -> 0%
where the time goes in v3:
time: 184 us
  blocking collectives  147 us (80%)
  Pallas kernels  25.9 us (14%)
  other arithmetic  4.69 us (3%)
  local copies, waits for them, and re-layouts  4.04 us (2%)
    all_to_all x4, blocking collectives, exchange(): return lax.all_to_all(pieces, axes, split_axis=0, concat_axis=0, tiled=True)  147 us
    pallas_call x1, Pallas kernels, solve_update(): pl.pallas_call(solve_kernel, in_specs=[pl.BlockSpec(memory_space=pltpu.VM...  19.4 us
    pallas_call x1, Pallas kernels, gram_pieces(): pl.pallas_call(lambda *refs: gram_kernel(scale, *refs), in_specs=[pl.Bloc...  3.79 us

profile of v3, /device:TPU:1, one launch (start us, length us, event | category | flops | bytes accessed | tf_op | source)
XLA Modules:
  0.0 183.6 jit_solution(8842620197431522567)
XLA Ops:
  0.6 0.1 fusion.15
  0.7 0.1 fusion.14
  0.8 0.7 compare_convert_fusion
  1.4 0.7 compare_select_fusion
  2.1 0.1 negate_multiply_fusion.1
  2.2 0.1 negate_multiply_fusion
  2.2 0.7 mul.351
  2.9 0.1 mul.352
  3.0 0.7 mul.359
  3.6 0.1 mul.360
  3.7 0.7 mul.367
  4.4 0.1 mul.368
  4.5 0.1 maximum_bitcast_fusion.2
  4.6 0.1 copy.25
  4.7 0.1 copy.26
  4.8 0.1 copy.27
  4.8 0.7 copy.19
  5.6 0.1 mul.364
  5.6 0.1 mul.365
  5.7 0.1 mul.356
  5.8 0.1 mul.357
  5.9 0.1 mul.348
  6.0 0.1 mul.349
  6.1 0.1 dot_general.8
  6.1 0.1 copy.23
  6.2 0.8 fusion.4
  7.1 0.9 fusion.6
  8.0 0.8 subtract_divide_fusion
  8.8 0.0 copy-start.2
  8.8 0.0 copy-start.3
  8.8 0.0 copy-start.1
  8.8 2.7 %dense_pieces.1 = f32[3072,128]{1,0:T(8,128)} custom-call(f32[6,65536]{1,0:T(8,128)} %jac_ref.1), custom_call_target="tpu_custom_call" | custom-call | tf_op jit(solution)/shard_map/dense_pieces/pallas_call | solution.py:111
  11.5 0.0 copy-start.4
  11.5 0.0 copy-start
  11.5 0.0 copy-done.2
  11.6 0.0 copy-done.3
  11.6 0.0 copy-done.1
  11.6 0.6 multiply_reduce_fusion
  12.2 0.2 multiply_reduce_fusion.2
  12.4 0.0 copy-done.4
  12.4 0.5 multiply_bitcast_fusion
  12.9 0.1 dynamic_update_slice.3.refs_2_
  13.0 0.0 copy-done
  13.0 92.5 %all_to_all.20 = f32[64,48,128]{2,1,0:T(8,128)S(1)} all-to-all(f32[64,48,128]{2,1,0:T(8,128)S(1)} %bitcast.55), channel_id=1, replica_groups=mesh['z'=16,'y'=4,'x'=4,'core'=2] {'z','y'}, dimensions={0} | all-to-all | bytes 3145728 | tf_op jit(solution)/shard_map/all_to_all | solution.py:288
  105.5 3.8 %gram_pieces.1 = (f32[768,128]{1,0:T(8,128)S(1)}, f32[384,1024]{1,0:T(8,128)S(1)}) custom-call(f32[3072,128]{1,0:T(8,128)S(1)} %bitcast.52, f32[1,1024]{1,0:T(1,128)} %prev_ref.1, f32[1,384]{1,0:T(1,128)S(1)} %dynamic_update_slice.3.refs_2_), custom_call_target="tpu_custom_call" | custom-call | tf_op jit(solution)/shard_map/gram_pieces/pallas_call | solution.py:170
  109.3 22.1 %all_to_all.21 = f32[32,24,128]{2,1,0:T(8,128)S(1)} all-to-all(f32[32,24,128]{2,1,0:T(8,128)S(1)} %bitcast.54), channel_id=1, replica_groups=mesh['z'=16,'y'=4,'x'=4,'core'=2] {'core','x','y'}, dimensions={0} | all-to-all | bytes 786432 | tf_op jit(solution)/shard_map/all_to_all | solution.py:288
  131.4 15.1 %all_to_all.22 = f32[16,24,128]{2,1,0:T(8,128)S(1)} all-to-all(f32[16,24,128]{2,1,0:T(8,128)S(1)} %broadcast_in_dim.7), channel_id=1, replica_groups=mesh['z'=16,'y'=4,'x'=4,'core'=2] {'z'}, dimensions={0} | all-to-all | bytes 393216 | tf_op jit(solution)/shard_map/all_to_all | solution.py:288
  146.6 17.6 %all_to_all.23 = f32[32,24,128]{2,1,0:T(8,128)S(1)} all-to-all(f32[32,24,128]{2,1,0:T(8,128)S(1)} %broadcast_in_dim.8), channel_id=1, replica_groups=mesh['z'=16,'y'=4,'x'=4,'core'=2] {'core','x','y'}, dimensions={0} | all-to-all | bytes 786432 | tf_op jit(solution)/shard_map/all_to_all | solution.py:288
  164.2 19.4 %solve_update.1 = f32[1,1024]{1,0:T(1,128)} custom-call(f32[768,128]{1,0:T(8,128)S(1)} %bitcast.53, f32[384,1024]{1,0:T(8,128)S(1)} %get-tuple-element.9.centred_ref, f32[1,1024]{1,0:T(1,128)} %prev_ref.1), custom_call_target="tpu_custom_call" | custom-call | tf_op jit(solution)/shard_map/solve_update/pallas_call | solution.py:278
  (15 shorter events, 0.3 us)
Async XLA Ops:
  8.8 2.8 %copy-start.2 = (f32[21,3]{0,1:T(4,128)S(1)}, f32[21,3]{0,1:T(4,128)}, u32[]{:S(2)}) copy-start(f32[21,3]{0,1:T(4,128)} %param.20) | copy-start | bytes 760
  8.8 2.7 %copy-start.3 = (f32[21,3]{0,1:T(4,128)S(1)}, f32[21,3]{0,1:T(4,128)}, u32[]{:S(2)}) copy-start(f32[21,3]{0,1:T(4,128)} %param.19) | copy-start | bytes 760
  8.8 2.8 %copy-start.1 = (f32[6,21,66,12]{2,1,3,0:T(8,128)S(1)}, f32[6,21,66,12]{2,1,3,0:T(8,128)}, u32[]{:S(2)}) copy-start(f32[6,21,66,12]{2,1,3,0:T(8,128)} %param.16) | copy-start | bytes 1197508
  11.5 0.9 copy-start.4
  11.5 1.5 copy-start

commit v4 on v3

--- a/solution.py
+++ b/solution.py
@@ -197,32 +197,41 @@
     )
 
 
+def reduce_panel(panel, first):
+    full = (SUB, BLOCK)
+    lane = lax.broadcasted_iota(jnp.int32, full, 1)
+    row_of = lax.broadcasted_iota(jnp.int32, full, 0)
+    pivots = [jnp.broadcast_to(panel[:, first + k : first + k + 1], full) for k in range(SUB)]
+    for k in range(SUB):
+        column = pivots[k]
+        scale = 1.0 / jnp.broadcast_to(column[k : k + 1, :], full)
+        mine = row_of == k
+        here = lane == first + k
+        row = jnp.broadcast_to(panel[k : k + 1, :], full)
+        row = jnp.where(here, scale, row * scale)
+        panel = jnp.where(mine, row, jnp.where(here, 0.0, panel) - column * row)
+        for j in range(k + 1, SUB):
+            other = jnp.broadcast_to(pivots[j][k : k + 1, :], full) * scale
+            pivots[j] = jnp.where(mine, other, pivots[j] - column * other)
+    return panel
+
+
 def inverse(block):
-    lane = lax.broadcasted_iota(jnp.int32, (SUB, BLOCK), 1)
-    row_of = lax.broadcasted_iota(jnp.int32, (SUB, BLOCK), 0)
-    lane_rest = lax.broadcasted_iota(jnp.int32, (BLOCK - SUB, BLOCK), 1)
     full = (SUB, BLOCK)
-
-    def step(_, value):
-        panel, rest = value[:SUB], value[SUB:]
-        columns = [rest[:, k : k + 1] for k in range(SUB)]
-        pivots = [jnp.broadcast_to(panel[:, k : k + 1], full) for k in range(SUB)]
-        for k in range(SUB):
-            column = pivots[k]
-            scale = 1.0 / jnp.broadcast_to(column[k : k + 1, :], full)
-            mine = row_of == k
-            row = jnp.broadcast_to(panel[k : k + 1, :], full)
-            row = jnp.where(lane == k, scale, row * scale)
-            panel = jnp.where(mine, row, jnp.where(lane == k, 0.0, panel) - column * row)
-            for j in range(k + 1, SUB):
-                other = jnp.broadcast_to(pivots[j][k : k + 1, :], full) * scale
-                pivots[j] = jnp.where(mine, other, pivots[j] - column * other)
-        rest = jnp.where(lane_rest < SUB, 0.0, rest)
-        for k in range(SUB):
-            rest = rest - columns[k] * panel[k : k + 1, :]
-        return pltpu.roll(jnp.concatenate([rest, panel], axis=0), BLOCK - SUB, 1)
-
-    return lax.fori_loop(0, BLOCK // SUB, step, block)
+    lane = lax.broadcasted_iota(jnp.int32, full, 1)
+    groups = [block[i : i + SUB] for i in range(0, BLOCK, SUB)]
+    for g, first in enumerate(range(0, BLOCK, SUB)):
+        panel = reduce_panel(groups[g], first)
+        rows = [jnp.broadcast_to(panel[k : k + 1, :], full) for k in range(SUB)]
+        here = (lane >= first) & (lane < first + SUB)
+        for i, value in enumerate(groups):
+            if i != g:
+                left = jnp.where(here, 0.0, value)
+                for k in range(SUB):
+                    left = left - value[:, first + k : first + k + 1] * rows[k]
+                groups[i] = left
+        groups[g] = panel
+    return jnp.concatenate(groups, axis=0)
 
 
 def solve_kernel(whole_ref, centred_ref, prev_ref, out_ref):
@@ -309,6 +318,8 @@
     rows, width = jacobian.shape
     walkers = rows * owners
     scale = 1.0 / (width * columns)
+    pieces = dense_pieces(jacobian, owners).reshape(owners, rows * SUB, LANES)
+    received = exchange(pieces, WALK)
     energy_mine = base_energy + nonlocal_energy(
         elec_pos, atom_pos, quad_ratio, rotation, channels, ecp_coef, ecp_expo
     )
@@ -317,9 +328,6 @@
         energy_mine[None, :] / columns,
         (0, lax.axis_index(WALK) * rows),
     )
-    pieces = dense_pieces(jacobian, owners).reshape(owners, rows * SUB, LANES)
-    pieces, energy_row = lax.optimization_barrier((pieces, energy_row))
-    received = exchange(pieces, WALK)
     packed, centred = gram_pieces(
         near(received.reshape(walkers * SUB, LANES)), prev_update, near(energy_row), walkers, scale
     )

time: 184 us -> 171 us (0.929)
  blocking collectives: 147 us -> 54.8 us
  waiting for transfers between devices: 0 us -> 69.6 us
  starting transfers between devices: 0 us -> 19.4 us
  Pallas kernels: 25.9 us -> 22.4 us
  other arithmetic: 4.69 us -> 2.01 us
  local copies, waits for them, and re-layouts: 4.04 us -> 1.4 us
    all_to_all x4 -> x3, blocking collectives: 147 us -> 54.8 us  [exchange(): return lax.all_to_all(pieces, axes, split_axis=0, concat_axis=0, tiled=True)]
    all_to_all x0 -> x1, waiting for transfers between devices: none -> 69.6 us  [exchange(): return lax.all_to_all(pieces, axes, split_axis=0, concat_axis=0, tiled=True)]
    all_to_all x0 -> x1, starting transfers between devices: none -> 19.4 us  [exchange(): return lax.all_to_all(pieces, axes, split_axis=0, concat_axis=0, tiled=True)]
    pallas_call x1, Pallas kernels: 19.4 us -> 16 us  [solve_update(): pl.pallas_call(solve_kernel, in_specs=[pl.BlockSpec(memory_space=pltpu.VM...]
  transfers between devices with their start and end apart: 0 -> 1, of which waited for: 0 -> 1; matrix products, arithmetic and copies ran while one was open for 0% -> 2% of each run, Pallas kernels for 0% -> 0%
where the time goes in v4:
time: 171 us
  waiting for transfers between devices  69.6 us (41%)
  blocking collectives  54.8 us (32%)
  Pallas kernels  22.4 us (13%)
  starting transfers between devices  19.4 us (11%)
  other arithmetic  2.01 us (1%)
    all_to_all x1, waiting for transfers between devices, exchange(): return lax.all_to_all(pieces, axes, split_axis=0, concat_axis=0, tiled=True)  69.6 us
    all_to_all x3, blocking collectives, exchange(): return lax.all_to_all(pieces, axes, split_axis=0, concat_axis=0, tiled=True)  54.8 us
    all_to_all x1, starting transfers between devices, exchange(): return lax.all_to_all(pieces, axes, split_axis=0, concat_axis=0, tiled=True)  19.4 us
    pallas_call x1, Pallas kernels, solve_update(): pl.pallas_call(solve_kernel, in_specs=[pl.BlockSpec(memory_space=pltpu.VM...  16 us
    pallas_call x1, Pallas kernels, gram_pieces(): pl.pallas_call(lambda *refs: gram_kernel(scale, *refs), in_specs=[pl.Bloc...  3.77 us
  transfers between devices with their start and end apart: 1, of which 1 were waited for; matrix products, arithmetic and copies ran while one was open for 2% of the time, Pallas kernels for 0%

profile of v4, /device:TPU:1, one launch (start us, length us, event | category | flops | bytes accessed | tf_op | source)
XLA Modules:
  0.0 170.8 jit_solution(1254369157318810046)
XLA Ops:
  0.6 2.6 %dense_pieces.1 = f32[3072,128]{1,0:T(8,128)} custom-call(f32[6,65536]{1,0:T(8,128)} %jac_ref.1), custom_call_target="tpu_custom_call" | custom-call | tf_op jit(solution)/shard_map/dense_pieces/pallas_call | solution.py:111
  3.3 0.0 copy-start.8
  3.3 0.0 copy-start.7
  3.3 0.0 copy-start.6
  3.3 0.0 copy-start.1
  3.3 0.0 copy-start.2
  3.3 0.0 copy-start.10
  3.3 0.0 copy-start.4
  3.3 0.0 copy-start.5
  3.3 0.0 copy-start.3
  3.3 19.4 %all-to-all-start = ((f32[64,48,128]{2,1,0:T(8,128)}), f32[64,48,128]{2,1,0:T(8,128)S(1)}, u32[]{:S(2)}, u32[]{:S(2)}) async-start(f32[64,48,128]{2,1,0:T(8,128)} %bitcast.55), calls=%async_computation | async-start | bytes 3145728 | tf_op jit(solution)/shard_map/all_to_all | solution.py:297
  22.8 0.0 copy-start
  22.8 0.0 copy-done.8
  22.8 0.1 mul.352
  22.9 0.0 copy-done.7
  22.9 0.1 mul.360
  23.0 0.0 copy-done.6
  23.0 0.1 mul.368
  23.1 0.1 fusion.15
  23.1 0.1 fusion.14
  23.2 0.1 negate_multiply_fusion.1
  23.3 0.1 negate_multiply_fusion
  23.4 0.1 maximum_bitcast_fusion.2
  23.5 0.1 copy.25
  23.6 0.1 copy.26
  23.7 0.1 copy.27
  23.7 0.0 copy-done.1
  23.7 0.1 mul.364
  23.8 0.1 mul.365
  23.9 0.1 mul.356
  24.0 0.1 mul.357
  24.1 0.1 mul.348
  24.2 0.1 mul.349
  24.3 0.1 dot_general.8
  24.3 0.1 copy.23
  24.4 0.0 copy-done.2
  24.4 0.1 fusion.4
  24.6 0.0 copy-done.10
  24.6 0.0 copy-done.4
  24.6 0.0 copy-done.5
  24.6 0.0 copy-start.9
  24.7 0.0 copy-done.3
  24.7 0.2 fusion.6
  24.9 0.1 subtract_divide_fusion
  25.0 0.0 copy-done
  25.0 0.6 multiply_reduce_fusion
  25.6 0.3 multiply_reduce_fusion.2
  25.9 0.0 copy-done.9
  25.9 0.5 multiply_bitcast_fusion
  26.4 0.1 dynamic_update_slice.3.refs_2_
  26.5 69.6 %all-to-all-done = f32[64,48,128]{2,1,0:T(8,128)S(1)} async-done(((f32[64,48,128]{2,1,0:T(8,128)}), f32[64,48,128]{2,1,0:T(8,128)S(1)}, u32[]{:S(2)}, u32[]{:S(2)}) %all-to-all-start) | async-done | bytes 1572896 | tf_op jit(solution)/shard_map/all_to_all | solution.py:297
  96.1 3.8 %gram_pieces.1 = (f32[768,128]{1,0:T(8,128)S(1)}, f32[384,1024]{1,0:T(8,128)S(1)}) custom-call(f32[3072,128]{1,0:T(8,128)S(1)} %bitcast.52, f32[1,1024]{1,0:T(1,128)} %prev_ref.1, f32[1,384]{1,0:T(1,128)S(1)} %dynamic_update_slice.3.refs_2_), custom_call_target="tpu_custom_call" | custom-call | tf_op jit(solution)/shard_map/gram_pieces/pallas_call | solution.py:170
  99.9 22.0 %all_to_all.20 = f32[32,24,128]{2,1,0:T(8,128)S(1)} all-to-all(f32[32,24,128]{2,1,0:T(8,128)S(1)} %bitcast.54), channel_id=1, replica_groups=mesh['z'=16,'y'=4,'x'=4,'core'=2] {'core','x','y'}, dimensions={0} | all-to-all | bytes 786432 | tf_op jit(solution)/shard_map/all_to_all | solution.py:297
  122.0 15.1 %all_to_all.21 = f32[16,24,128]{2,1,0:T(8,128)S(1)} all-to-all(f32[16,24,128]{2,1,0:T(8,128)S(1)} %broadcast_in_dim.7), channel_id=1, replica_groups=mesh['z'=16,'y'=4,'x'=4,'core'=2] {'z'}, dimensions={0} | all-to-all | bytes 393216 | tf_op jit(solution)/shard_map/all_to_all | solution.py:297
  137.2 17.6 %all_to_all.22 = f32[32,24,128]{2,1,0:T(8,128)S(1)} all-to-all(f32[32,24,128]{2,1,0:T(8,128)S(1)} %broadcast_in_dim.8), channel_id=1, replica_groups=mesh['z'=16,'y'=4,'x'=4,'core'=2] {'core','x','y'}, dimensions={0} | all-to-all | bytes 786432 | tf_op jit(solution)/shard_map/all_to_all | solution.py:297
  154.8 16.0 %solve_update.1 = f32[1,1024]{1,0:T(1,128)} custom-call(f32[768,128]{1,0:T(8,128)S(1)} %bitcast.53, f32[384,1024]{1,0:T(8,128)S(1)} %get-tuple-element.5.centred_ref, f32[1,1024]{1,0:T(1,128)} %prev_ref.1), custom_call_target="tpu_custom_call" | custom-call | tf_op jit(solution)/shard_map/solve_update/pallas_call | solution.py:287
  (21 shorter events, 0.3 us)
Async XLA Ops:
  3.3 19.5 %copy-start.8 = (f32[12]{0:T(128)S(1)}, f32[12]{0:T(128)}, u32[]{:S(2)}) copy-start(f32[12]{0:T(128)} %constant.69) | copy-start | bytes 148
  3.3 19.6 %copy-start.7 = (f32[12]{0:T(128)S(1)}, f32[12]{0:T(128)}, u32[]{:S(2)}) copy-start(f32[12]{0:T(128)} %constant.71) | copy-start | bytes 148
  3.3 19.7 %copy-start.6 = (f32[12]{0:T(128)S(1)}, f32[12]{0:T(128)}, u32[]{:S(2)}) copy-start(f32[12]{0:T(128)} %constant.73) | copy-start | bytes 148
  3.3 20.5 %copy-start.1 = (f32[6,3,66]{2,1,0:T(4,128)S(1)}, f32[6,3,66]{2,1,0:T(4,128)}, u32[]{:S(2)}) copy-start(f32[6,3,66]{2,1,0:T(4,128)} %param.14) | copy-start | bytes 14260
  3.3 21.2 %copy-start.2 = (f32[3,21]{1,0:T(4,128)S(1)}, f32[3,21]{1,0:T(4,128)}, u32[]{:S(2)}) copy-start(f32[3,21]{1,0:T(4,128)} %param.15) | copy-start | bytes 760
  3.3 21.3 %copy-start.10 = (s32[21]{0:T(128)S(1)}, s32[21]{0:T(128)}, u32[]{:S(2)}) copy-start(s32[21]{0:T(128)} %param.18) | copy-start | bytes 256
  3.3 21.3 %copy-start.4 = (f32[21,3]{0,1:T(4,128)S(1)}, f32[21,3]{0,1:T(4,128)}, u32[]{:S(2)}) copy-start(f32[21,3]{0,1:T(4,128)} %param.20) | copy-start | bytes 760
  3.3 21.3 %copy-start.5 = (f32[21,3]{0,1:T(4,128)S(1)}, f32[21,3]{0,1:T(4,128)}, u32[]{:S(2)}) copy-start(f32[21,3]{0,1:T(4,128)} %param.19) | copy-start | bytes 760
  3.3 21.3 %copy-start.3 = (s32[6,66]{1,0:T(8,128)S(1)}, s32[6,66]{1,0:T(8,128)}, u32[]{:S(2)}) copy-start(s32[6,66]{1,0:T(8,128)} %param.17) | copy-start | bytes 4756
  3.3 92.8 %all-to-all-start = ((f32[64,48,128]{2,1,0:T(8,128)}), f32[64,48,128]{2,1,0:T(8,128)S(1)}, u32[]{:S(2)}, u32[]{:S(2)}) async-start(f32[64,48,128]{2,1,0:T(8,128)} %bitcast.55), calls=%async_computation | async-start | bytes 3145728 | tf_op jit(solution)/shard_map/all_to_all | solution.py:297
  22.8 2.3 %copy-start = (f32[6,21,66,12]{2,1,3,0:T(8,128)S(1)}, f32[6,21,66,12]{2,1,3,0:T(8,128)}, u32[]{:S(2)}) copy-start(f32[6,21,66,12]{2,1,3,0:T(8,128)} %param.16) | copy-start | bytes 1197508
  24.6 1.2 copy-start.9

commit v5 on v4

--- a/solution.py
+++ b/solution.py
@@ -87,6 +87,7 @@
 
 BLOCK = 128
 HALF = 64
+EXTRA = 16
 SUB = 8
 LANES = 128
 WALK = ("z", "y")
@@ -124,39 +125,45 @@
     return high, low
 
 
-def contract_last(left, right, precision=None):
+def contract_last(left, right):
     return lax.dot_general(
         left,
         right,
         (((1,), (1,)), ((), ())),
-        precision=precision,
         preferred_element_type=jnp.float32,
     )
 
 
-def gram_kernel(scale, x_ref, prev_ref, energy_ref, packed_ref, centred_ref, high_ref, low_ref):
+def gram_kernel(scale, x_ref, prev_ref, energy_ref, packed_ref, centred_ref):
     walkers = centred_ref.shape[0]
-    for sub in range(SUB):
-        part = x_ref[pl.ds(sub, walkers, stride=SUB), :]
-        part = part - jnp.sum(part, axis=0, keepdims=True) * (1.0 / walkers)
-        lanes = slice(sub * LANES, (sub + 1) * LANES)
-        centred_ref[:, lanes] = part
-        high, low = split_high_low(part)
-        high_ref[:, lanes] = high
-        low_ref[:, lanes] = low
     blocks = walkers // BLOCK
+    prev_parts = split_high_low(prev_ref[...])
+    strips = [None] * blocks
+    for sub in range(0, SUB, 2):
+        parts = []
+        for s in (sub, sub + 1):
+            part = x_ref[pl.ds(s, walkers, stride=SUB), :]
+            part = part - jnp.sum(part, axis=0, keepdims=True) * (1.0 / walkers)
+            centred_ref[:, s * LANES : (s + 1) * LANES] = part
+            parts.append(part)
+        high, low = split_high_low(jnp.concatenate(parts, axis=1))
+        lanes = slice(sub * LANES, (sub + 2) * LANES)
+        for i in range(blocks):
+            left = [part[i * BLOCK : (i + 1) * BLOCK] for part in (high, low)]
+            if i == 0:
+                extra = [jnp.broadcast_to(p[:, lanes], (EXTRA, 2 * LANES)) for p in prev_parts]
+                left = [jnp.concatenate(pair, axis=0) for pair in zip(left, extra)]
+            strip = contract_last(left[0], high[i * BLOCK :])
+            strip = strip + contract_last(left[0], low[i * BLOCK :])
+            strip = strip + contract_last(left[1], high[i * BLOCK :])
+            strips[i] = strip if strips[i] is None else strips[i] + strip
     row = 0
     for i in range(blocks):
-        mine = slice(i * BLOCK, (i + 1) * BLOCK)
-        rest = slice(i * BLOCK, walkers)
-        strip = contract_last(high_ref[mine, :], high_ref[rest, :])
-        strip = strip + contract_last(high_ref[mine, :], low_ref[rest, :])
-        strip = strip + contract_last(low_ref[mine, :], high_ref[rest, :])
-        strip = strip * scale
+        strip = strips[i] * scale
         for j in range(blocks - i):
-            packed_ref[row : row + BLOCK, :] = strip[:, j * BLOCK : (j + 1) * BLOCK]
+            packed_ref[row : row + BLOCK, :] = strip[:BLOCK, j * BLOCK : (j + 1) * BLOCK]
             row += BLOCK
-    along = contract_last(prev_ref[...], centred_ref[...], lax.Precision.HIGHEST) * scale
+    along = strips[0][BLOCK : BLOCK + 1, :] * scale
     for j in range(walkers // HALF):
         part = slice(j * HALF, (j + 1) * HALF)
         packed_ref[HALF + j : HALF + j + 1, :HALF] = along[:, part]
@@ -175,10 +182,6 @@
             pltpu.VMEM((pieces * BLOCK, LANES), jnp.float32),
             pltpu.VMEM((walkers, width), jnp.float32),
         ),
-        scratch_shapes=[
-            pltpu.VMEM((walkers, width), jnp.bfloat16),
-            pltpu.VMEM((walkers, width), jnp.bfloat16),
-        ],
         name="gram_pieces",
     )(received, prev_update, energy_row)
 
@@ -224,12 +227,11 @@
         panel = reduce_panel(groups[g], first)
         rows = [jnp.broadcast_to(panel[k : k + 1, :], full) for k in range(SUB)]
         here = (lane >= first) & (lane < first + SUB)
-        for i, value in enumerate(groups):
-            if i != g:
-                left = jnp.where(here, 0.0, value)
-                for k in range(SUB):
-                    left = left - value[:, first + k : first + k + 1] * rows[k]
-                groups[i] = left
+        for i in [*range(g + 1, len(groups)), *range(g)]:
+            left = jnp.where(here, 0.0, groups[i])
+            for k in range(SUB):
+                left = left - groups[i][:, first + k : first + k + 1] * rows[k]
+            groups[i] = left
         groups[g] = panel
     return jnp.concatenate(groups, axis=0)
 
@@ -271,16 +273,19 @@
     s22 = s22 - matmul(s12, w12, 0, 0)
     y1 = matmul(r1, inv1)
     r2 = r2 - matmul(y1, s12)
+    y0 = y0 - matmul(y1, w01, 1, 1)
+    w02 = w02 - matmul(w01, w12)
     inv2 = inverse(s22)
     x2 = matmul(r2, inv2)
     x1 = y1 - matmul(x2, w12, 1, 1)
-    x0 = y0 - matmul(x1, w01, 1, 1) - matmul(x2, w02, 1, 1)
-    out_ref[...] = (
-        matmul(x0, centred_ref[0:BLOCK, :])
-        + matmul(x1, centred_ref[BLOCK : 2 * BLOCK, :])
-        + matmul(x2, centred_ref[2 * BLOCK :, :])
-        + momentum * prev_ref[...]
-    )
+    x0 = y0 - matmul(x2, w02, 1, 1)
+    total = jnp.zeros((SUB, out_ref.shape[1]), jnp.float32)
+    for i, solved in enumerate((x0, x1, x2)):
+        solved = jnp.broadcast_to(solved, (BLOCK, BLOCK))
+        column = jnp.sum(jnp.where(lane == row_of, solved, 0.0), axis=1, keepdims=True)
+        terms = centred_ref[i * BLOCK : (i + 1) * BLOCK, :] * column
+        total = total + jnp.sum(terms.reshape(BLOCK // SUB, SUB, -1), axis=0)
+    out_ref[...] = jnp.sum(total, axis=0, keepdims=True) + momentum * prev_ref[...]
 
 
 def solve_update(whole, centred, prev_update):

time: 171 us -> 169 us (0.988)
  Pallas kernels: 22.4 us -> 19.8 us
where the time goes in v5:
time: 169 us; the launch traced here: 168 us
  waiting for transfers between devices  69.6 us (41%)
  blocking collectives  54.8 us (32%)
  Pallas kernels  19.8 us (12%)
  starting transfers between devices  19.4 us (11%)
  other arithmetic  2.01 us (1%)
    all_to_all x1, waiting for transfers between devices, exchange(): return lax.all_to_all(pieces, axes, split_axis=0, concat_axis=0, tiled=True)  69.6 us
    all_to_all x3, blocking collectives, exchange(): return lax.all_to_all(pieces, axes, split_axis=0, concat_axis=0, tiled=True)  54.8 us
    all_to_all x1, starting transfers between devices, exchange(): return lax.all_to_all(pieces, axes, split_axis=0, concat_axis=0, tiled=True)  19.4 us
    pallas_call x1, Pallas kernels, solve_update(): pl.pallas_call(solve_kernel, in_specs=[pl.BlockSpec(memory_space=pltpu.VM...  14.9 us
  transfers between devices with their start and end apart: 1, of which 1 were waited for; matrix products, arithmetic and copies ran while one was open for 2% of the time, Pallas kernels for 0%

profile of v5, /device:TPU:1, one launch (start us, length us, event | category | flops | bytes accessed | tf_op | source)
XLA Modules:
  0.0 168.2 jit_solution(17968327619124765383)
XLA Ops:
  0.6 2.6 %dense_pieces.1 = f32[3072,128]{1,0:T(8,128)} custom-call(f32[6,65536]{1,0:T(8,128)} %jac_ref.1), custom_call_target="tpu_custom_call" | custom-call | tf_op jit(solution)/shard_map/dense_pieces/pallas_call | solution.py:112
  3.3 0.0 copy-start.8
  3.3 0.0 copy-start.7
  3.3 0.0 copy-start.6
  3.3 0.0 copy-start.1
  3.3 0.0 copy-start.2
  3.3 0.0 copy-start.10
  3.3 0.0 copy-start.4
  3.3 0.0 copy-start.5
  3.3 0.0 copy-start.3
  3.3 19.4 %all-to-all-start = ((f32[64,48,128]{2,1,0:T(8,128)}), f32[64,48,128]{2,1,0:T(8,128)S(1)}, u32[]{:S(2)}, u32[]{:S(2)}) async-start(f32[64,48,128]{2,1,0:T(8,128)} %bitcast.55), calls=%async_computation | async-start | bytes 3145728 | tf_op jit(solution)/shard_map/all_to_all | solution.py:302
  22.8 0.0 copy-start
  22.8 0.0 copy-done.8
  22.8 0.1 mul.352
  22.9 0.0 copy-done.7
  22.9 0.1 mul.360
  23.0 0.0 copy-done.6
  23.0 0.1 mul.368
  23.1 0.1 fusion.15
  23.1 0.1 fusion.14
  23.2 0.1 negate_multiply_fusion.1
  23.3 0.1 negate_multiply_fusion
  23.4 0.1 maximum_bitcast_fusion.2
  23.5 0.1 copy.25
  23.6 0.1 copy.26
  23.7 0.1 copy.27
  23.7 0.0 copy-done.1
  23.7 0.1 mul.364
  23.8 0.1 mul.365
  23.9 0.1 mul.356
  24.0 0.1 mul.357
  24.1 0.1 mul.348
  24.2 0.1 mul.349
  24.3 0.1 dot_general.8
  24.3 0.1 copy.23
  24.4 0.0 copy-done.2
  24.4 0.1 fusion.4
  24.6 0.0 copy-done.10
  24.6 0.0 copy-done.4
  24.6 0.0 copy-done.5
  24.6 0.0 copy-start.9
  24.7 0.0 copy-done.3
  24.7 0.2 fusion.6
  24.9 0.1 subtract_divide_fusion
  25.0 0.0 copy-done
  25.0 0.6 multiply_reduce_fusion
  25.6 0.3 multiply_reduce_fusion.2
  25.9 0.0 copy-done.9
  25.9 0.5 multiply_bitcast_fusion
  26.4 0.1 dynamic_update_slice.3.refs_2_
  26.5 69.6 %all-to-all-done = f32[64,48,128]{2,1,0:T(8,128)S(1)} async-done(((f32[64,48,128]{2,1,0:T(8,128)}), f32[64,48,128]{2,1,0:T(8,128)S(1)}, u32[]{:S(2)}, u32[]{:S(2)}) %all-to-all-start) | async-done | bytes 1572896 | tf_op jit(solution)/shard_map/all_to_all | solution.py:302
  96.1 2.3 %gram_pieces.1 = (f32[768,128]{1,0:T(8,128)S(1)}, f32[384,1024]{1,0:T(8,128)S(1)}) custom-call(f32[3072,128]{1,0:T(8,128)S(1)} %bitcast.52, f32[1,1024]{1,0:T(1,128)} %prev_ref.1, f32[1,384]{1,0:T(1,128)S(1)} %dynamic_update_slice.3.refs_2_), custom_call_target="tpu_custom_call" | custom-call | tf_op jit(solution)/shard_map/gram_pieces/pallas_call | solution.py:177
  98.4 22.0 %all_to_all.20 = f32[32,24,128]{2,1,0:T(8,128)S(1)} all-to-all(f32[32,24,128]{2,1,0:T(8,128)S(1)} %bitcast.54), channel_id=1, replica_groups=mesh['z'=16,'y'=4,'x'=4,'core'=2] {'core','x','y'}, dimensions={0} | all-to-all | bytes 786432 | tf_op jit(solution)/shard_map/all_to_all | solution.py:302
  120.5 15.1 %all_to_all.21 = f32[16,24,128]{2,1,0:T(8,128)S(1)} all-to-all(f32[16,24,128]{2,1,0:T(8,128)S(1)} %broadcast_in_dim.7), channel_id=1, replica_groups=mesh['z'=16,'y'=4,'x'=4,'core'=2] {'z'}, dimensions={0} | all-to-all | bytes 393216 | tf_op jit(solution)/shard_map/all_to_all | solution.py:302
  135.7 17.6 %all_to_all.22 = f32[32,24,128]{2,1,0:T(8,128)S(1)} all-to-all(f32[32,24,128]{2,1,0:T(8,128)S(1)} %broadcast_in_dim.8), channel_id=1, replica_groups=mesh['z'=16,'y'=4,'x'=4,'core'=2] {'core','x','y'}, dimensions={0} | all-to-all | bytes 786432 | tf_op jit(solution)/shard_map/all_to_all | solution.py:302
  153.3 14.9 %solve_update.1 = f32[1,1024]{1,0:T(1,128)} custom-call(f32[768,128]{1,0:T(8,128)S(1)} %bitcast.53, f32[384,1024]{1,0:T(8,128)S(1)} %get-tuple-element.5.centred_ref, f32[1,1024]{1,0:T(1,128)} %prev_ref.1), custom_call_target="tpu_custom_call" | custom-call | tf_op jit(solution)/shard_map/solve_update/pallas_call | solution.py:292
  (21 shorter events, 0.3 us)
Async XLA Ops:
  3.3 19.5 %copy-start.8 = (f32[12]{0:T(128)S(1)}, f32[12]{0:T(128)}, u32[]{:S(2)}) copy-start(f32[12]{0:T(128)} %constant.69) | copy-start | bytes 148
  3.3 19.6 %copy-start.7 = (f32[12]{0:T(128)S(1)}, f32[12]{0:T(128)}, u32[]{:S(2)}) copy-start(f32[12]{0:T(128)} %constant.71) | copy-start | bytes 148
  3.3 19.7 %copy-start.6 = (f32[12]{0:T(128)S(1)}, f32[12]{0:T(128)}, u32[]{:S(2)}) copy-start(f32[12]{0:T(128)} %constant.73) | copy-start | bytes 148
  3.3 20.5 %copy-start.1 = (f32[6,3,66]{2,1,0:T(4,128)S(1)}, f32[6,3,66]{2,1,0:T(4,128)}, u32[]{:S(2)}) copy-start(f32[6,3,66]{2,1,0:T(4,128)} %param.14) | copy-start | bytes 14260
  3.3 21.2 %copy-start.2 = (f32[3,21]{1,0:T(4,128)S(1)}, f32[3,21]{1,0:T(4,128)}, u32[]{:S(2)}) copy-start(f32[3,21]{1,0:T(4,128)} %param.15) | copy-start | bytes 760
  3.3 21.3 %copy-start.10 = (s32[21]{0:T(128)S(1)}, s32[21]{0:T(128)}, u32[]{:S(2)}) copy-start(s32[21]{0:T(128)} %param.18) | copy-start | bytes 256
  3.3 21.3 %copy-start.4 = (f32[21,3]{0,1:T(4,128)S(1)}, f32[21,3]{0,1:T(4,128)}, u32[]{:S(2)}) copy-start(f32[21,3]{0,1:T(4,128)} %param.20) | copy-start | bytes 760
  3.3 21.3 %copy-start.5 = (f32[21,3]{0,1:T(4,128)S(1)}, f32[21,3]{0,1:T(4,128)}, u32[]{:S(2)}) copy-start(f32[21,3]{0,1:T(4,128)} %param.19) | copy-start | bytes 760
  3.3 21.3 %copy-start.3 = (s32[6,66]{1,0:T(8,128)S(1)}, s32[6,66]{1,0:T(8,128)}, u32[]{:S(2)}) copy-start(s32[6,66]{1,0:T(8,128)} %param.17) | copy-start | bytes 4756
  3.3 92.8 %all-to-all-start = ((f32[64,48,128]{2,1,0:T(8,128)}), f32[64,48,128]{2,1,0:T(8,128)S(1)}, u32[]{:S(2)}, u32[]{:S(2)}) async-start(f32[64,48,128]{2,1,0:T(8,128)} %bitcast.55), calls=%async_computation | async-start | bytes 3145728 | tf_op jit(solution)/shard_map/all_to_all | solution.py:302
  22.8 2.3 %copy-start = (f32[6,21,66,12]{2,1,3,0:T(8,128)S(1)}, f32[6,21,66,12]{2,1,3,0:T(8,128)}, u32[]{:S(2)}) copy-start(f32[6,21,66,12]{2,1,3,0:T(8,128)} %param.16) | copy-start | bytes 1197508
  24.6 1.2 copy-start.9

commit v6 on v5

--- a/solution.py
+++ b/solution.py
@@ -95,26 +95,38 @@
 PLANE = ("core", "x", "y")
 
 
-def spread_rows(jac_ref, out_ref):
-    rows = jac_ref.shape[0]
-    for tile in range(jac_ref.shape[1] // LANES):
-        owner, sub = divmod(tile, SUB)
-        out_ref[pl.ds(owner * rows * SUB + sub, rows, stride=SUB), :] = jac_ref[
-            :, tile * LANES : (tile + 1) * LANES
-        ]
+def spread_rows(jac_ref, out_ref, buffer_ref, sems):
+    rows, width = jac_ref.shape
+    chunks = sems.shape[0]
+    part = width // chunks
+    copies = []
+    for c in range(chunks):
+        lanes = slice(c * part, (c + 1) * part)
+        copy = pltpu.make_async_copy(jac_ref.at[:, lanes], buffer_ref.at[:, lanes], sems.at[c])
+        copy.start()
+        copies.append(copy)
+    for c in range(chunks):
+        copies[c].wait()
+        for tile in range(c * part // LANES, (c + 1) * part // LANES):
+            owner, sub = divmod(tile, SUB)
+            out_ref[pl.ds(owner * rows * SUB + sub, rows, stride=SUB), :] = buffer_ref[
+                :, tile * LANES : (tile + 1) * LANES
+            ]
 
 
 def dense_pieces(jacobian, owners):
     rows, width = jacobian.shape
-    steps = 2
-    piece = width // owners
-    assert piece == SUB * LANES
+    chunks = 8
+    assert width // owners == SUB * LANES
     return pl.pallas_call(
         spread_rows,
-        grid=(steps,),
-        in_specs=[pl.BlockSpec((rows, width // steps), lambda i: (0, i))],
-        out_specs=pl.BlockSpec((owners // steps * rows * SUB, LANES), lambda i: (i, 0)),
-        out_shape=jax.ShapeDtypeStruct((owners * rows * SUB, LANES), jnp.float32),
+        in_specs=[pl.BlockSpec(memory_space=pl.ANY)],
+        out_specs=pl.BlockSpec(memory_space=pltpu.VMEM),
+        out_shape=pltpu.VMEM((owners * rows * SUB, LANES), jnp.float32),
+        scratch_shapes=[
+            pltpu.VMEM((rows, width), jnp.float32),
+            pltpu.SemaphoreType.DMA((chunks,)),
+        ],
         name="dense_pieces",
     )(jacobian)
 
@@ -190,12 +202,19 @@
     return pltpu.with_memory_space_constraint(value, pltpu.VMEM)
 
 
+def split_three(value):
+    high, low = split_high_low(value)
+    rest = value - high.astype(jnp.float32)
+    return high, low, (rest - low.astype(jnp.float32)).astype(jnp.bfloat16)
+
+
 def matmul(left, right, left_dim=1, right_dim=0):
+    lh, lm, ll = split_three(left)
+    rh, rm, rl = split_three(right)
     return lax.dot_general(
-        left,
-        right,
+        jnp.concatenate([lh, lh, lm, lm, lh, ll], axis=left_dim),
+        jnp.concatenate([rh, rm, rh, rm, rl, rh], axis=right_dim),
         (((left_dim,), (right_dim,)), ((), ())),
-        precision=lax.Precision.HIGHEST,
         preferred_element_type=jnp.float32,
     )
 

time: 169 us -> 169 us (level)
  no operation moved by 1% of the time
where the time goes in v6:
time: 169 us; the launch traced here: 168 us
  waiting for transfers between devices  69.6 us (41%)
  blocking collectives  54.8 us (32%)
  Pallas kernels  19.7 us (12%)
  starting transfers between devices  19.4 us (11%)
  other arithmetic  2.01 us (1%)
    all_to_all x1, waiting for transfers between devices, exchange(): return lax.all_to_all(pieces, axes, split_axis=0, concat_axis=0, tiled=True)  69.6 us
    all_to_all x3, blocking collectives, exchange(): return lax.all_to_all(pieces, axes, split_axis=0, concat_axis=0, tiled=True)  54.8 us
    all_to_all x1, starting transfers between devices, exchange(): return lax.all_to_all(pieces, axes, split_axis=0, concat_axis=0, tiled=True)  19.4 us
    pallas_call x1, Pallas kernels, solve_update(): pl.pallas_call(solve_kernel, in_specs=[pl.BlockSpec(memory_space=pltpu.VM...  14.6 us
  transfers between devices with their start and end apart: 1, of which 1 were waited for; matrix products, arithmetic and copies ran while one was open for 2% of the time, Pallas kernels for 0%

profile of v6, /device:TPU:1, one launch (start us, length us, event | category | flops | bytes accessed | tf_op | source)
XLA Modules:
  0.0 168.1 jit_solution(4789003035179175098)
XLA Ops:
  0.6 2.8 %dense_pieces.1 = f32[3072,128]{1,0:T(8,128)} custom-call(f32[6,65536]{1,0:T(8,128)} %jac_ref.1), custom_call_target="tpu_custom_call" | custom-call | tf_op jit(solution)/shard_map/dense_pieces/pallas_call | solution.py:121
  3.4 0.0 copy-start.8
  3.4 0.0 copy-start.7
  3.4 0.0 copy-start.6
  3.4 0.0 copy-start.1
  3.5 0.0 copy-start.2
  3.5 0.0 copy-start.10
  3.5 0.0 copy-start.4
  3.5 0.0 copy-start.5
  3.5 0.0 copy-start.3
  3.5 19.4 %all-to-all-start = ((f32[64,48,128]{2,1,0:T(8,128)}), f32[64,48,128]{2,1,0:T(8,128)S(1)}, u32[]{:S(2)}, u32[]{:S(2)}) async-start(f32[64,48,128]{2,1,0:T(8,128)} %bitcast.22), calls=%async_computation | async-start | bytes 3145728 | tf_op jit(solution)/shard_map/all_to_all | solution.py:321
  22.9 0.0 copy-start
  23.0 0.0 copy-done.8
  23.0 0.1 mul.352
  23.1 0.0 copy-done.7
  23.1 0.1 mul.360
  23.2 0.0 copy-done.6
  23.2 0.1 mul.368
  23.3 0.1 fusion.15
  23.3 0.1 fusion.14
  23.4 0.1 negate_multiply_fusion.1
  23.5 0.1 negate_multiply_fusion
  23.6 0.1 maximum_bitcast_fusion.2
  23.7 0.1 copy.25
  23.8 0.1 copy.26
  23.8 0.1 copy.27
  23.9 0.0 copy-done.1
  23.9 0.1 mul.364
  24.0 0.1 mul.365
  24.1 0.1 mul.356
  24.2 0.1 mul.357
  24.2 0.1 mul.348
  24.3 0.1 mul.349
  24.4 0.1 dot_general.8
  24.5 0.1 copy.23
  24.6 0.0 copy-done.2
  24.6 0.1 fusion.4
  24.7 0.0 copy-done.10
  24.8 0.0 copy-done.4
  24.8 0.0 copy-done.5
  24.8 0.0 copy-start.9
  24.8 0.0 copy-done.3
  24.9 0.2 fusion.6
  25.1 0.1 subtract_divide_fusion
  25.2 0.0 copy-done
  25.2 0.6 multiply_reduce_fusion
  25.8 0.3 multiply_reduce_fusion.2
  26.0 0.0 copy-done.9
  26.0 0.5 multiply_bitcast_fusion
  26.6 0.1 dynamic_update_slice.3.refs_2_
  26.6 69.6 %all-to-all-done = f32[64,48,128]{2,1,0:T(8,128)S(1)} async-done(((f32[64,48,128]{2,1,0:T(8,128)}), f32[64,48,128]{2,1,0:T(8,128)S(1)}, u32[]{:S(2)}, u32[]{:S(2)}) %all-to-all-start) | async-done | bytes 1572896 | tf_op jit(solution)/shard_map/all_to_all | solution.py:321
  96.3 2.3 %gram_pieces.1 = (f32[768,128]{1,0:T(8,128)S(1)}, f32[384,1024]{1,0:T(8,128)S(1)}) custom-call(f32[3072,128]{1,0:T(8,128)S(1)} %bitcast.52, f32[1,1024]{1,0:T(1,128)} %prev_ref.1, f32[1,384]{1,0:T(1,128)S(1)} %dynamic_update_slice.3.refs_2_), custom_call_target="tpu_custom_call" | custom-call | tf_op jit(solution)/shard_map/gram_pieces/pallas_call | solution.py:189
  98.6 22.0 %all_to_all.20 = f32[32,24,128]{2,1,0:T(8,128)S(1)} all-to-all(f32[32,24,128]{2,1,0:T(8,128)S(1)} %bitcast.54), channel_id=1, replica_groups=mesh['z'=16,'y'=4,'x'=4,'core'=2] {'core','x','y'}, dimensions={0} | all-to-all | bytes 786432 | tf_op jit(solution)/shard_map/all_to_all | solution.py:321
  120.7 15.1 %all_to_all.21 = f32[16,24,128]{2,1,0:T(8,128)S(1)} all-to-all(f32[16,24,128]{2,1,0:T(8,128)S(1)} %broadcast_in_dim.7), channel_id=1, replica_groups=mesh['z'=16,'y'=4,'x'=4,'core'=2] {'z'}, dimensions={0} | all-to-all | bytes 393216 | tf_op jit(solution)/shard_map/all_to_all | solution.py:321
  135.9 17.6 %all_to_all.22 = f32[32,24,128]{2,1,0:T(8,128)S(1)} all-to-all(f32[32,24,128]{2,1,0:T(8,128)S(1)} %broadcast_in_dim.8), channel_id=1, replica_groups=mesh['z'=16,'y'=4,'x'=4,'core'=2] {'core','x','y'}, dimensions={0} | all-to-all | bytes 786432 | tf_op jit(solution)/shard_map/all_to_all | solution.py:321
  153.5 14.6 %solve_update.1 = f32[1,1024]{1,0:T(1,128)} custom-call(f32[768,128]{1,0:T(8,128)S(1)} %bitcast.53, f32[384,1024]{1,0:T(8,128)S(1)} %get-tuple-element.5.centred_ref, f32[1,1024]{1,0:T(1,128)} %prev_ref.1), custom_call_target="tpu_custom_call" | custom-call | tf_op jit(solution)/shard_map/solve_update/pallas_call | solution.py:311
  (21 shorter events, 0.3 us)
Async XLA Ops:
  3.4 19.6 %copy-start.8 = (f32[12]{0:T(128)S(1)}, f32[12]{0:T(128)}, u32[]{:S(2)}) copy-start(f32[12]{0:T(128)} %constant.69) | copy-start | bytes 148
  3.4 19.7 %copy-start.7 = (f32[12]{0:T(128)S(1)}, f32[12]{0:T(128)}, u32[]{:S(2)}) copy-start(f32[12]{0:T(128)} %constant.71) | copy-start | bytes 148
  3.4 19.7 %copy-start.6 = (f32[12]{0:T(128)S(1)}, f32[12]{0:T(128)}, u32[]{:S(2)}) copy-start(f32[12]{0:T(128)} %constant.73) | copy-start | bytes 148
  3.4 20.5 %copy-start.1 = (f32[6,3,66]{2,1,0:T(4,128)S(1)}, f32[6,3,66]{2,1,0:T(4,128)}, u32[]{:S(2)}) copy-start(f32[6,3,66]{2,1,0:T(4,128)} %param.14) | copy-start | bytes 14260
  3.5 21.2 %copy-start.2 = (f32[3,21]{1,0:T(4,128)S(1)}, f32[3,21]{1,0:T(4,128)}, u32[]{:S(2)}) copy-start(f32[3,21]{1,0:T(4,128)} %param.15) | copy-start | bytes 760
  3.5 21.3 %copy-start.10 = (s32[21]{0:T(128)S(1)}, s32[21]{0:T(128)}, u32[]{:S(2)}) copy-start(s32[21]{0:T(128)} %param.18) | copy-start | bytes 256
  3.5 21.3 %copy-start.4 = (f32[21,3]{0,1:T(4,128)S(1)}, f32[21,3]{0,1:T(4,128)}, u32[]{:S(2)}) copy-start(f32[21,3]{0,1:T(4,128)} %param.20) | copy-start | bytes 760
  3.5 21.3 %copy-start.5 = (f32[21,3]{0,1:T(4,128)S(1)}, f32[21,3]{0,1:T(4,128)}, u32[]{:S(2)}) copy-start(f32[21,3]{0,1:T(4,128)} %param.19) | copy-start | bytes 760
  3.5 21.3 %copy-start.3 = (s32[6,66]{1,0:T(8,128)S(1)}, s32[6,66]{1,0:T(8,128)}, u32[]{:S(2)}) copy-start(s32[6,66]{1,0:T(8,128)} %param.17) | copy-start | bytes 4756
  3.5 92.8 %all-to-all-start = ((f32[64,48,128]{2,1,0:T(8,128)}), f32[64,48,128]{2,1,0:T(8,128)S(1)}, u32[]{:S(2)}, u32[]{:S(2)}) async-start(f32[64,48,128]{2,1,0:T(8,128)} %bitcast.22), calls=%async_computation | async-start | bytes 3145728 | tf_op jit(solution)/shard_map/all_to_all | solution.py:321
  22.9 2.2 %copy-start = (f32[6,21,66,12]{2,1,3,0:T(8,128)S(1)}, f32[6,21,66,12]{2,1,3,0:T(8,128)}, u32[]{:S(2)}) copy-start(f32[6,21,66,12]{2,1,3,0:T(8,128)} %param.16) | copy-start | bytes 1197508
  24.8 1.2 copy-start.9

commit v7 on v6

--- a/solution.py
+++ b/solution.py
@@ -92,39 +92,51 @@
 LANES = 128
 WALK = ("z", "y")
 COL = ("x", "core")
-PLANE = ("core", "x", "y")
-
-
-def spread_rows(jac_ref, out_ref, buffer_ref, sems):
+PLANE = ("y", "core", "x")
+
+
+def spread_rows(jac_ref, out_ref, taken_ref, spread_ref, in_sems, out_sems):
     rows, width = jac_ref.shape
-    chunks = sems.shape[0]
-    part = width // chunks
-    copies = []
+    chunks = in_sems.shape[0]
+    lanes, height = width // chunks, out_ref.shape[0] // chunks
+    copies_in, copies_out = [], []
     for c in range(chunks):
-        lanes = slice(c * part, (c + 1) * part)
-        copy = pltpu.make_async_copy(jac_ref.at[:, lanes], buffer_ref.at[:, lanes], sems.at[c])
+        part = slice(c * lanes, (c + 1) * lanes)
+        copies_in.append(
+            pltpu.make_async_copy(jac_ref.at[:, part], taken_ref.at[:, part], in_sems.at[c])
+        )
+        part = slice(c * height, (c + 1) * height)
+        copies_out.append(
+            pltpu.make_async_copy(spread_ref.at[part], out_ref.at[part], out_sems.at[c])
+        )
+    for copy in copies_in:
         copy.start()
-        copies.append(copy)
     for c in range(chunks):
-        copies[c].wait()
-        for tile in range(c * part // LANES, (c + 1) * part // LANES):
+        copies_in[c].wait()
+        for tile in range(c * lanes // LANES, (c + 1) * lanes // LANES):
             owner, sub = divmod(tile, SUB)
-            out_ref[pl.ds(owner * rows * SUB + sub, rows, stride=SUB), :] = buffer_ref[
+            spread_ref[pl.ds(owner * rows * SUB + sub, rows, stride=SUB), :] = taken_ref[
                 :, tile * LANES : (tile + 1) * LANES
             ]
+        copies_out[c].start()
+    for copy in copies_out:
+        copy.wait()
 
 
 def dense_pieces(jacobian, owners):
     rows, width = jacobian.shape
     chunks = 8
     assert width // owners == SUB * LANES
+    shape = (owners * rows * SUB, LANES)
     return pl.pallas_call(
         spread_rows,
         in_specs=[pl.BlockSpec(memory_space=pl.ANY)],
-        out_specs=pl.BlockSpec(memory_space=pltpu.VMEM),
-        out_shape=pltpu.VMEM((owners * rows * SUB, LANES), jnp.float32),
+        out_specs=pl.BlockSpec(memory_space=pl.ANY),
+        out_shape=jax.ShapeDtypeStruct(shape, jnp.float32),
         scratch_shapes=[
             pltpu.VMEM((rows, width), jnp.float32),
+            pltpu.VMEM(shape, jnp.float32),
+            pltpu.SemaphoreType.DMA((chunks,)),
             pltpu.SemaphoreType.DMA((chunks,)),
         ],
         name="dense_pieces",
@@ -255,6 +267,10 @@
     return jnp.concatenate(groups, axis=0)
 
 
+def row_sums(block, row):
+    return jnp.sum(block * row, axis=1, keepdims=True)
+
+
 def solve_kernel(whole_ref, centred_ref, prev_ref, out_ref):
     lane = lax.broadcasted_iota(jnp.int32, (BLOCK, BLOCK), 1)
     row_of = lax.broadcasted_iota(jnp.int32, (BLOCK, BLOCK), 0)
@@ -292,16 +308,18 @@
     s22 = s22 - matmul(s12, w12, 0, 0)
     y1 = matmul(r1, inv1)
     r2 = r2 - matmul(y1, s12)
-    y0 = y0 - matmul(y1, w01, 1, 1)
     w02 = w02 - matmul(w01, w12)
+    column0 = row_sums(inv0, right[0]) - row_sums(w01, y1)
+    column1 = row_sums(inv1, r1)
     inv2 = inverse(s22)
     x2 = matmul(r2, inv2)
-    x1 = y1 - matmul(x2, w12, 1, 1)
-    x0 = y0 - matmul(x2, w02, 1, 1)
+    solved = (
+        column0 - row_sums(w02, x2),
+        column1 - row_sums(w12, x2),
+        row_sums(inv2, r2),
+    )
     total = jnp.zeros((SUB, out_ref.shape[1]), jnp.float32)
-    for i, solved in enumerate((x0, x1, x2)):
-        solved = jnp.broadcast_to(solved, (BLOCK, BLOCK))
-        column = jnp.sum(jnp.where(lane == row_of, solved, 0.0), axis=1, keepdims=True)
+    for i, column in enumerate(solved):
         terms = centred_ref[i * BLOCK : (i + 1) * BLOCK, :] * column
         total = total + jnp.sum(terms.reshape(BLOCK // SUB, SUB, -1), axis=0)
     out_ref[...] = jnp.sum(total, axis=0, keepdims=True) + momentum * prev_ref[...]

time: 169 us -> 168 us (level)
  no operation moved by 1% of the time
where the time goes in v7:
time: 168 us
  waiting for transfers between devices  69.6 us (41%)
  blocking collectives  55.1 us (33%)
  starting transfers between devices  19.4 us (12%)
  Pallas kernels  19.2 us (11%)
  other arithmetic  2.01 us (1%)
    all_to_all x1, waiting for transfers between devices, exchange(): return lax.all_to_all(pieces, axes, split_axis=0, concat_axis=0, tiled=True)  69.6 us
    all_to_all x3, blocking collectives, exchange(): return lax.all_to_all(pieces, axes, split_axis=0, concat_axis=0, tiled=True)  55.1 us
    all_to_all x1, starting transfers between devices, exchange(): return lax.all_to_all(pieces, axes, split_axis=0, concat_axis=0, tiled=True)  19.4 us
    pallas_call x1, Pallas kernels, solve_update(): pl.pallas_call(solve_kernel, in_specs=[pl.BlockSpec(memory_space=pltpu.VM...  14.5 us
  transfers between devices with their start and end apart: 1, of which 1 were waited for; matrix products, arithmetic and copies ran while one was open for 2% of the time, Pallas kernels for 0%

profile of v7, /device:TPU:1, one launch (start us, length us, event | category | flops | bytes accessed | tf_op | source)
XLA Modules:
  0.0 168.0 jit_solution(2417652184121778868)
XLA Ops:
  0.6 2.4 %dense_pieces.1 = f32[3072,128]{1,0:T(8,128)} custom-call(f32[6,65536]{1,0:T(8,128)} %jac_ref.1), custom_call_target="tpu_custom_call" | custom-call | tf_op jit(solution)/shard_map/dense_pieces/pallas_call | solution.py:131
  3.0 0.0 copy-start.8
  3.0 0.0 copy-start.7
  3.0 0.0 copy-start.6
  3.1 0.0 copy-start.1
  3.1 0.0 copy-start.2
  3.1 0.0 copy-start.10
  3.1 0.0 copy-start.4
  3.1 0.0 copy-start.5
  3.1 0.0 copy-start.3
  3.1 19.4 %all-to-all-start = ((f32[64,48,128]{2,1,0:T(8,128)}), f32[64,48,128]{2,1,0:T(8,128)S(1)}, u32[]{:S(2)}, u32[]{:S(2)}) async-start(f32[64,48,128]{2,1,0:T(8,128)} %bitcast.55), calls=%async_computation | async-start | bytes 3145728 | tf_op jit(solution)/shard_map/all_to_all | solution.py:339
  22.6 0.0 copy-start
  22.6 0.0 copy-done.8
  22.6 0.1 mul.352
  22.7 0.0 copy-done.7
  22.7 0.1 mul.360
  22.8 0.0 copy-done.6
  22.8 0.1 mul.368
  22.9 0.1 fusion.15
  22.9 0.1 fusion.14
  23.0 0.1 negate_multiply_fusion.1
  23.1 0.1 negate_multiply_fusion
  23.2 0.1 maximum_bitcast_fusion.2
  23.3 0.1 copy.25
  23.4 0.1 copy.26
  23.4 0.1 copy.27
  23.5 0.0 copy-done.1
  23.5 0.1 mul.364
  23.6 0.1 mul.365
  23.7 0.1 mul.356
  23.8 0.1 mul.357
  23.9 0.1 mul.348
  23.9 0.1 mul.349
  24.0 0.1 dot_general.8
  24.1 0.1 copy.23
  24.2 0.0 copy-done.2
  24.2 0.1 fusion.4
  24.3 0.0 copy-done.10
  24.4 0.0 copy-done.4
  24.4 0.0 copy-done.5
  24.4 0.0 copy-start.9
  24.5 0.0 copy-done.3
  24.5 0.2 fusion.6
  24.7 0.1 subtract_divide_fusion
  24.8 0.0 copy-done
  24.8 0.6 multiply_reduce_fusion
  25.4 0.3 multiply_reduce_fusion.2
  25.6 0.0 copy-done.9
  25.6 0.5 multiply_bitcast_fusion
  26.2 0.1 dynamic_update_slice.3.refs_2_
  26.3 69.6 %all-to-all-done = f32[64,48,128]{2,1,0:T(8,128)S(1)} async-done(((f32[64,48,128]{2,1,0:T(8,128)}), f32[64,48,128]{2,1,0:T(8,128)S(1)}, u32[]{:S(2)}, u32[]{:S(2)}) %all-to-all-start) | async-done | bytes 1572896 | tf_op jit(solution)/shard_map/all_to_all | solution.py:339
  95.9 2.3 %gram_pieces.1 = (f32[768,128]{1,0:T(8,128)S(1)}, f32[384,1024]{1,0:T(8,128)S(1)}) custom-call(f32[3072,128]{1,0:T(8,128)S(1)} %bitcast.52, f32[1,1024]{1,0:T(1,128)} %prev_ref.1, f32[1,384]{1,0:T(1,128)S(1)} %dynamic_update_slice.3.refs_2_), custom_call_target="tpu_custom_call" | custom-call | tf_op jit(solution)/shard_map/gram_pieces/pallas_call | solution.py:201
  98.2 22.2 %all_to_all.20 = f32[32,24,128]{2,1,0:T(8,128)S(1)} all-to-all(f32[32,24,128]{2,1,0:T(8,128)S(1)} %bitcast.54), channel_id=1, replica_groups=mesh['z'=16,'y'=4,'x'=4,'core'=2] {'y','core','x'}, dimensions={0} | all-to-all | bytes 786432 | tf_op jit(solution)/shard_map/all_to_all | solution.py:339
  120.5 15.8 %all_to_all.21 = f32[16,24,128]{2,1,0:T(8,128)S(1)} all-to-all(f32[16,24,128]{2,1,0:T(8,128)S(1)} %broadcast_in_dim.7), channel_id=1, replica_groups=mesh['z'=16,'y'=4,'x'=4,'core'=2] {'z'}, dimensions={0} | all-to-all | bytes 393216 | tf_op jit(solution)/shard_map/all_to_all | solution.py:339
  136.4 17.0 %all_to_all.22 = f32[32,24,128]{2,1,0:T(8,128)S(1)} all-to-all(f32[32,24,128]{2,1,0:T(8,128)S(1)} %broadcast_in_dim.8), channel_id=1, replica_groups=mesh['z'=16,'y'=4,'x'=4,'core'=2] {'y','core','x'}, dimensions={0} | all-to-all | bytes 786432 | tf_op jit(solution)/shard_map/all_to_all | solution.py:339
  153.4 14.5 %solve_update.1 = f32[1,1024]{1,0:T(1,128)} custom-call(f32[768,128]{1,0:T(8,128)S(1)} %bitcast.53, f32[384,1024]{1,0:T(8,128)S(1)} %get-tuple-element.5.centred_ref, f32[1,1024]{1,0:T(1,128)} %prev_ref.1), custom_call_target="tpu_custom_call" | custom-call | tf_op jit(solution)/shard_map/solve_update/pallas_call | solution.py:329
  (21 shorter events, 0.3 us)
Async XLA Ops:
  3.0 19.6 %copy-start.8 = (f32[12]{0:T(128)S(1)}, f32[12]{0:T(128)}, u32[]{:S(2)}) copy-start(f32[12]{0:T(128)} %constant.69) | copy-start | bytes 148
  3.0 19.7 %copy-start.7 = (f32[12]{0:T(128)S(1)}, f32[12]{0:T(128)}, u32[]{:S(2)}) copy-start(f32[12]{0:T(128)} %constant.71) | copy-start | bytes 148
  3.0 19.7 %copy-start.6 = (f32[12]{0:T(128)S(1)}, f32[12]{0:T(128)}, u32[]{:S(2)}) copy-start(f32[12]{0:T(128)} %constant.73) | copy-start | bytes 148
  3.1 20.5 %copy-start.1 = (f32[6,3,66]{2,1,0:T(4,128)S(1)}, f32[6,3,66]{2,1,0:T(4,128)}, u32[]{:S(2)}) copy-start(f32[6,3,66]{2,1,0:T(4,128)} %param.14) | copy-start | bytes 14260
  3.1 21.2 %copy-start.2 = (f32[3,21]{1,0:T(4,128)S(1)}, f32[3,21]{1,0:T(4,128)}, u32[]{:S(2)}) copy-start(f32[3,21]{1,0:T(4,128)} %param.15) | copy-start | bytes 760
  3.1 21.3 %copy-start.10 = (s32[21]{0:T(128)S(1)}, s32[21]{0:T(128)}, u32[]{:S(2)}) copy-start(s32[21]{0:T(128)} %param.18) | copy-start | bytes 256
  3.1 21.3 %copy-start.4 = (f32[21,3]{0,1:T(4,128)S(1)}, f32[21,3]{0,1:T(4,128)}, u32[]{:S(2)}) copy-start(f32[21,3]{0,1:T(4,128)} %param.20) | copy-start | bytes 760
  3.1 21.3 %copy-start.5 = (f32[21,3]{0,1:T(4,128)S(1)}, f32[21,3]{0,1:T(4,128)}, u32[]{:S(2)}) copy-start(f32[21,3]{0,1:T(4,128)} %param.19) | copy-start | bytes 760
  3.1 21.3 %copy-start.3 = (s32[6,66]{1,0:T(8,128)S(1)}, s32[6,66]{1,0:T(8,128)}, u32[]{:S(2)}) copy-start(s32[6,66]{1,0:T(8,128)} %param.17) | copy-start | bytes 4756
  3.1 92.8 %all-to-all-start = ((f32[64,48,128]{2,1,0:T(8,128)}), f32[64,48,128]{2,1,0:T(8,128)S(1)}, u32[]{:S(2)}, u32[]{:S(2)}) async-start(f32[64,48,128]{2,1,0:T(8,128)} %bitcast.55), calls=%async_computation | async-start | bytes 3145728 | tf_op jit(solution)/shard_map/all_to_all | solution.py:339
  22.6 2.2 %copy-start = (f32[6,21,66,12]{2,1,3,0:T(8,128)S(1)}, f32[6,21,66,12]{2,1,3,0:T(8,128)}, u32[]{:S(2)}) copy-start(f32[6,21,66,12]{2,1,3,0:T(8,128)} %param.16) | copy-start | bytes 1197508
  24.4 1.2 copy-start.9

commit v8 on v7

--- a/solution.py
+++ b/solution.py
@@ -88,11 +88,12 @@
 BLOCK = 128
 HALF = 64
 EXTRA = 16
+PANEL = 16
 SUB = 8
 LANES = 128
 WALK = ("z", "y")
 COL = ("x", "core")
-PLANE = ("y", "core", "x")
+PLANE = ("core", "x", "y")
 
 
 def spread_rows(jac_ref, out_ref, taken_ref, spread_ref, in_sems, out_sems):
@@ -232,11 +233,11 @@
 
 
 def reduce_panel(panel, first):
-    full = (SUB, BLOCK)
+    full = (PANEL, BLOCK)
     lane = lax.broadcasted_iota(jnp.int32, full, 1)
     row_of = lax.broadcasted_iota(jnp.int32, full, 0)
-    pivots = [jnp.broadcast_to(panel[:, first + k : first + k + 1], full) for k in range(SUB)]
-    for k in range(SUB):
+    pivots = [jnp.broadcast_to(panel[:, first + k : first + k + 1], full) for k in range(PANEL)]
+    for k in range(PANEL):
         column = pivots[k]
         scale = 1.0 / jnp.broadcast_to(column[k : k + 1, :], full)
         mine = row_of == k
@@ -244,31 +245,27 @@
         row = jnp.broadcast_to(panel[k : k + 1, :], full)
         row = jnp.where(here, scale, row * scale)
         panel = jnp.where(mine, row, jnp.where(here, 0.0, panel) - column * row)
-        for j in range(k + 1, SUB):
+        for j in range(k + 1, PANEL):
             other = jnp.broadcast_to(pivots[j][k : k + 1, :], full) * scale
             pivots[j] = jnp.where(mine, other, pivots[j] - column * other)
     return panel
 
 
 def inverse(block):
-    full = (SUB, BLOCK)
+    full = (PANEL, BLOCK)
     lane = lax.broadcasted_iota(jnp.int32, full, 1)
-    groups = [block[i : i + SUB] for i in range(0, BLOCK, SUB)]
-    for g, first in enumerate(range(0, BLOCK, SUB)):
+    groups = [block[i : i + PANEL] for i in range(0, BLOCK, PANEL)]
+    for g, first in enumerate(range(0, BLOCK, PANEL)):
         panel = reduce_panel(groups[g], first)
-        rows = [jnp.broadcast_to(panel[k : k + 1, :], full) for k in range(SUB)]
-        here = (lane >= first) & (lane < first + SUB)
+        rows = [jnp.broadcast_to(panel[k : k + 1, :], full) for k in range(PANEL)]
+        here = (lane >= first) & (lane < first + PANEL)
         for i in [*range(g + 1, len(groups)), *range(g)]:
             left = jnp.where(here, 0.0, groups[i])
-            for k in range(SUB):
+            for k in range(PANEL):
                 left = left - groups[i][:, first + k : first + k + 1] * rows[k]
             groups[i] = left
         groups[g] = panel
     return jnp.concatenate(groups, axis=0)
-
-
-def row_sums(block, row):
-    return jnp.sum(block * row, axis=1, keepdims=True)
 
 
 def solve_kernel(whole_ref, centred_ref, prev_ref, out_ref):
@@ -308,18 +305,16 @@
     s22 = s22 - matmul(s12, w12, 0, 0)
     y1 = matmul(r1, inv1)
     r2 = r2 - matmul(y1, s12)
+    y0 = y0 - matmul(y1, w01, 1, 1)
     w02 = w02 - matmul(w01, w12)
-    column0 = row_sums(inv0, right[0]) - row_sums(w01, y1)
-    column1 = row_sums(inv1, r1)
     inv2 = inverse(s22)
     x2 = matmul(r2, inv2)
-    solved = (
-        column0 - row_sums(w02, x2),
-        column1 - row_sums(w12, x2),
-        row_sums(inv2, r2),
-    )
+    x1 = y1 - matmul(x2, w12, 1, 1)
+    x0 = y0 - matmul(x2, w02, 1, 1)
     total = jnp.zeros((SUB, out_ref.shape[1]), jnp.float32)
-    for i, column in enumerate(solved):
+    for i, solved in enumerate((x0, x1, x2)):
+        solved = jnp.broadcast_to(solved, (BLOCK, BLOCK))
+        column = jnp.sum(jnp.where(lane == row_of, solved, 0.0), axis=1, keepdims=True)
         terms = centred_ref[i * BLOCK : (i + 1) * BLOCK, :] * column
         total = total + jnp.sum(terms.reshape(BLOCK // SUB, SUB, -1), axis=0)
     out_ref[...] = jnp.sum(total, axis=0, keepdims=True) + momentum * prev_ref[...]

time: 168 us -> 168 us (level)
  no operation moved by 1% of the time
where the time goes in v8:
time: 168 us; the launch traced here: 167 us
  waiting for transfers between devices  69.6 us (41%)
  blocking collectives  54.7 us (33%)
  starting transfers between devices  19.4 us (12%)
  Pallas kernels  18.8 us (11%)
  other arithmetic  2.01 us (1%)
    all_to_all x1, waiting for transfers between devices, exchange(): return lax.all_to_all(pieces, axes, split_axis=0, concat_axis=0, tiled=True)  69.6 us
    all_to_all x3, blocking collectives, exchange(): return lax.all_to_all(pieces, axes, split_axis=0, concat_axis=0, tiled=True)  54.7 us
    all_to_all x1, starting transfers between devices, exchange(): return lax.all_to_all(pieces, axes, split_axis=0, concat_axis=0, tiled=True)  19.4 us
    pallas_call x1, Pallas kernels, solve_update(): pl.pallas_call(solve_kernel, in_specs=[pl.BlockSpec(memory_space=pltpu.VM...  14.1 us
  transfers between devices with their start and end apart: 1, of which 1 were waited for; matrix products, arithmetic and copies ran while one was open for 2% of the time, Pallas kernels for 0%

profile of v8, /device:TPU:1, one launch (start us, length us, event | category | flops | bytes accessed | tf_op | source)
XLA Modules:
  0.0 167.2 jit_solution(10677344206969369570)
XLA Ops:
  0.6 2.4 %dense_pieces.1 = f32[3072,128]{1,0:T(8,128)} custom-call(f32[6,65536]{1,0:T(8,128)} %jac_ref.1), custom_call_target="tpu_custom_call" | custom-call | tf_op jit(solution)/shard_map/dense_pieces/pallas_call | solution.py:132
  3.0 0.0 copy-start.8
  3.0 0.0 copy-start.7
  3.0 0.0 copy-start.6
  3.1 0.0 copy-start.1
  3.1 0.0 copy-start.2
  3.1 0.0 copy-start.10
  3.1 0.0 copy-start.4
  3.1 0.0 copy-start.5
  3.1 0.0 copy-start.3
  3.1 19.4 %all-to-all-start = ((f32[64,48,128]{2,1,0:T(8,128)}), f32[64,48,128]{2,1,0:T(8,128)S(1)}, u32[]{:S(2)}, u32[]{:S(2)}) async-start(f32[64,48,128]{2,1,0:T(8,128)} %bitcast.55), calls=%async_computation | async-start | bytes 3145728 | tf_op jit(solution)/shard_map/all_to_all | solution.py:334
  22.6 0.0 copy-start
  22.6 0.0 copy-done.8
  22.6 0.1 mul.352
  22.7 0.0 copy-done.7
  22.7 0.1 mul.360
  22.8 0.0 copy-done.6
  22.8 0.1 mul.368
  22.9 0.1 fusion.15
  22.9 0.1 fusion.14
  23.0 0.1 negate_multiply_fusion.1
  23.1 0.1 negate_multiply_fusion
  23.2 0.1 maximum_bitcast_fusion.2
  23.3 0.1 copy.25
  23.4 0.1 copy.26
  23.4 0.1 copy.27
  23.5 0.0 copy-done.1
  23.5 0.1 mul.364
  23.6 0.1 mul.365
  23.7 0.1 mul.356
  23.8 0.1 mul.357
  23.9 0.1 mul.348
  23.9 0.1 mul.349
  24.0 0.1 dot_general.8
  24.1 0.1 copy.23
  24.2 0.0 copy-done.2
  24.2 0.1 fusion.4
  24.3 0.0 copy-done.10
  24.4 0.0 copy-done.4
  24.4 0.0 copy-done.5
  24.4 0.0 copy-start.9
  24.5 0.0 copy-done.3
  24.5 0.2 fusion.6
  24.7 0.1 subtract_divide_fusion
  24.8 0.0 copy-done
  24.8 0.6 multiply_reduce_fusion
  25.4 0.3 multiply_reduce_fusion.2
  25.6 0.0 copy-done.9
  25.6 0.5 multiply_bitcast_fusion
  26.2 0.1 dynamic_update_slice.3.refs_2_
  26.3 69.6 %all-to-all-done = f32[64,48,128]{2,1,0:T(8,128)S(1)} async-done(((f32[64,48,128]{2,1,0:T(8,128)}), f32[64,48,128]{2,1,0:T(8,128)S(1)}, u32[]{:S(2)}, u32[]{:S(2)}) %all-to-all-start) | async-done | bytes 1572896 | tf_op jit(solution)/shard_map/all_to_all | solution.py:334
  95.9 2.3 %gram_pieces.1 = (f32[768,128]{1,0:T(8,128)S(1)}, f32[384,1024]{1,0:T(8,128)S(1)}) custom-call(f32[3072,128]{1,0:T(8,128)S(1)} %bitcast.52, f32[1,1024]{1,0:T(1,128)} %prev_ref.1, f32[1,384]{1,0:T(1,128)S(1)} %dynamic_update_slice.3.refs_2_), custom_call_target="tpu_custom_call" | custom-call | tf_op jit(solution)/shard_map/gram_pieces/pallas_call | solution.py:202
  98.2 22.0 %all_to_all.20 = f32[32,24,128]{2,1,0:T(8,128)S(1)} all-to-all(f32[32,24,128]{2,1,0:T(8,128)S(1)} %bitcast.54), channel_id=1, replica_groups=mesh['z'=16,'y'=4,'x'=4,'core'=2] {'core','x','y'}, dimensions={0} | all-to-all | bytes 786432 | tf_op jit(solution)/shard_map/all_to_all | solution.py:334
  120.3 15.1 %all_to_all.21 = f32[16,24,128]{2,1,0:T(8,128)S(1)} all-to-all(f32[16,24,128]{2,1,0:T(8,128)S(1)} %broadcast_in_dim.7), channel_id=1, replica_groups=mesh['z'=16,'y'=4,'x'=4,'core'=2] {'z'}, dimensions={0} | all-to-all | bytes 393216 | tf_op jit(solution)/shard_map/all_to_all | solution.py:334
  135.5 17.6 %all_to_all.22 = f32[32,24,128]{2,1,0:T(8,128)S(1)} all-to-all(f32[32,24,128]{2,1,0:T(8,128)S(1)} %broadcast_in_dim.8), channel_id=1, replica_groups=mesh['z'=16,'y'=4,'x'=4,'core'=2] {'core','x','y'}, dimensions={0} | all-to-all | bytes 786432 | tf_op jit(solution)/shard_map/all_to_all | solution.py:334
  153.1 14.1 %solve_update.1 = f32[1,1024]{1,0:T(1,128)} custom-call(f32[768,128]{1,0:T(8,128)S(1)} %bitcast.53, f32[384,1024]{1,0:T(8,128)S(1)} %get-tuple-element.5.centred_ref, f32[1,1024]{1,0:T(1,128)} %prev_ref.1), custom_call_target="tpu_custom_call" | custom-call | tf_op jit(solution)/shard_map/solve_update/pallas_call | solution.py:324
  (21 shorter events, 0.3 us)
Async XLA Ops:
  3.0 19.6 %copy-start.8 = (f32[12]{0:T(128)S(1)}, f32[12]{0:T(128)}, u32[]{:S(2)}) copy-start(f32[12]{0:T(128)} %constant.69) | copy-start | bytes 148
  3.0 19.7 %copy-start.7 = (f32[12]{0:T(128)S(1)}, f32[12]{0:T(128)}, u32[]{:S(2)}) copy-start(f32[12]{0:T(128)} %constant.71) | copy-start | bytes 148
  3.0 19.7 %copy-start.6 = (f32[12]{0:T(128)S(1)}, f32[12]{0:T(128)}, u32[]{:S(2)}) copy-start(f32[12]{0:T(128)} %constant.73) | copy-start | bytes 148
  3.1 20.5 %copy-start.1 = (f32[6,3,66]{2,1,0:T(4,128)S(1)}, f32[6,3,66]{2,1,0:T(4,128)}, u32[]{:S(2)}) copy-start(f32[6,3,66]{2,1,0:T(4,128)} %param.14) | copy-start | bytes 14260
  3.1 21.2 %copy-start.2 = (f32[3,21]{1,0:T(4,128)S(1)}, f32[3,21]{1,0:T(4,128)}, u32[]{:S(2)}) copy-start(f32[3,21]{1,0:T(4,128)} %param.15) | copy-start | bytes 760
  3.1 21.3 %copy-start.10 = (s32[21]{0:T(128)S(1)}, s32[21]{0:T(128)}, u32[]{:S(2)}) copy-start(s32[21]{0:T(128)} %param.18) | copy-start | bytes 256
  3.1 21.3 %copy-start.4 = (f32[21,3]{0,1:T(4,128)S(1)}, f32[21,3]{0,1:T(4,128)}, u32[]{:S(2)}) copy-start(f32[21,3]{0,1:T(4,128)} %param.20) | copy-start | bytes 760
  3.1 21.3 %copy-start.5 = (f32[21,3]{0,1:T(4,128)S(1)}, f32[21,3]{0,1:T(4,128)}, u32[]{:S(2)}) copy-start(f32[21,3]{0,1:T(4,128)} %param.19) | copy-start | bytes 760
  3.1 21.3 %copy-start.3 = (s32[6,66]{1,0:T(8,128)S(1)}, s32[6,66]{1,0:T(8,128)}, u32[]{:S(2)}) copy-start(s32[6,66]{1,0:T(8,128)} %param.17) | copy-start | bytes 4756
  3.1 92.8 %all-to-all-start = ((f32[64,48,128]{2,1,0:T(8,128)}), f32[64,48,128]{2,1,0:T(8,128)S(1)}, u32[]{:S(2)}, u32[]{:S(2)}) async-start(f32[64,48,128]{2,1,0:T(8,128)} %bitcast.55), calls=%async_computation | async-start | bytes 3145728 | tf_op jit(solution)/shard_map/all_to_all | solution.py:334
  22.6 2.2 %copy-start = (f32[6,21,66,12]{2,1,3,0:T(8,128)S(1)}, f32[6,21,66,12]{2,1,3,0:T(8,128)}, u32[]{:S(2)}) copy-start(f32[6,21,66,12]{2,1,3,0:T(8,128)} %param.16) | copy-start | bytes 1197508
  24.4 1.2 copy-start.9
